TPU v7x, 256 devices: a whole 4x4x8 slice. The times are simulated.
256 devices in a mesh: ctx: 32 (over x_lo, z, core), tp: 8 (over y, x_hi).
Axes of the slice: x: 4 (x_hi: 2, x_lo: 2; x = x_hi * 2 + x_lo), y: 4, z: 8, core: 2. Of those that a mesh axis runs over, the one named last changes fastest.
Arguments:
- q_in: float32 [16384, 2048], P('ctx', 'tp'), may hold values from -6 to 6
- k_in: float32 [16384, 2048], P('ctx', 'tp'), may hold values from -6 to 6
- v_in: float32 [16384, 2048], P('ctx', 'tp'), may hold values from -6 to 6
- short_taps: float32 [3, 3, 2048], P(None, None, 'tp'), may hold values from -3.5 to 3.5
- long_filter: float32 [16384, 2048], P('ctx', 'tp'), may hold values from -6 to 6
- skip_gain: float32 [2048], P('tp'), may hold values from 0.5 to 1.5
- conv_saved: float32 [16384, 2048], P('ctx', 'tp'), may hold values from -6 to 6
- grad_out: float32 [16384, 2048], P('ctx', 'tp'), may hold values from -6 to 6
Outputs:
- grad_q: float32 [16384, 2048], P('ctx', 'tp')
- grad_k: float32 [16384, 2048], P('ctx', 'tp')
- grad_v: float32 [16384, 2048], P('ctx', 'tp')
- grad_filter: float32 [2048, 16384], P(('ctx', 'tp'))
- grad_taps: float32 [3, 3, 2048], P(None, None, 'tp')
- grad_skip: float32 [2048], P('tp')
All inputs are finite; a program needn't handle non-finite values.
Results may differ from a plain program's by a relative error of at most 0.00018.
Values sent between devices are 32-bit elements; how exact they have to be, the bound alone decides.
No kernel may reach another device: no remote copies, remote signals or barrier semaphores. Data moves between devices by JAX's collectives and lax.ppermute only.
A program may use at most 128 MiB of HBM per device.

v0:
```python
import functools
import math

import jax
import jax.numpy as jnp
import numpy as np
from jax import lax
from jax.experimental import pallas as pl
from jax.experimental.pallas import tpu as pltpu
from jax.sharding import PartitionSpec as P


f32, bf16 = jnp.float32, jnp.bfloat16
LANES = 128


def target_of(c, t):
    x_lo, zp, par, core = c >> 4, (c >> 2) & 3, (c >> 1) & 1, c & 1
    ahead = (t - zp) & 3
    far, kind = ahead >> 1, ahead & 1
    spread = far ^ core ^ (par if kind else 0)
    new_par = far if kind else par ^ far
    across = (t >> 2) ^ x_lo ^ core
    return 4 * t + 2 * new_par + core, across * 4 + kind * 2 + spread


def owner_of(group, t):
    new_par, core, target = group >> 4, (group >> 3) & 1, group & 7
    across, kind, spread = target >> 2, (target >> 1) & 1, target & 1
    far = new_par if kind else spread ^ core
    par = far ^ core ^ spread if kind else new_par ^ far
    zp = (t - (2 * far + kind)) & 3
    x_lo = (t >> 2) ^ across ^ core
    return x_lo * 16 + zp * 4 + par * 2 + core


def halves(table):
    table = np.asarray(table, np.float64).astype(np.float32)
    high = table.astype(bf16)
    low = (table - high.astype(np.float32)).astype(bf16)
    return high, low


@functools.cache
def tables(blocks, scale):
    total = 2 * blocks * 4 * LANES
    rows = np.arange(4 * blocks)
    a = (rows % blocks) * 4 + rows // blocks
    q = np.arange(LANES) + 0.5
    l = np.arange(LANES)
    ang = 2 * np.pi * np.outer(q, a) / (total // LANES)
    outer = np.concatenate([np.cos(ang), -np.sin(ang)], 0)
    back = scale * np.concatenate([np.cos(ang), -np.sin(ang)], 0).T
    ang = 2 * np.pi * np.outer(q, l) / total
    twist_re, twist_im = np.cos(ang).astype(np.float32), -np.sin(ang).astype(np.float32)
    ang = 2 * np.pi * (np.outer(l, l) % LANES) / LANES
    co, si = np.cos(ang), np.sin(ang)
    inner = np.block([[co, -si], [si, co]])
    inner_back = np.block([[co, si], [-si, co]])
    oh, ol = halves(outer)
    bh, bl = halves(back)
    ih, il = halves(inner)
    jh, jl = halves(inner_back)
    ol = np.concatenate([ol[:LANES], ol[LANES:]], 1)
    big = np.concatenate([np.concatenate([oh, oh], 1), ih, il, jh, jl, bh, bl, ol], 0)
    return big, np.concatenate([twist_re, twist_im], 0)


def split(x):
    high = x.astype(bf16)
    return high, (x - high.astype(f32)).astype(bf16)


def mm(a, b):
    return jnp.dot(a, b, preferred_element_type=f32)


def load_pair(src_a, src_b, row_a, row_b, blocks):
    def one(src, row):
        return jnp.concatenate(
            [src[pl.ds(i * 8 + row, blocks, stride=32), :] for i in range(4)], axis=0
        )

    return jnp.concatenate([one(src_a, row_a), one(src_b, row_b)], axis=1)


def forward(pair, tab, twist):
    high, low = split(pair)
    ol = jnp.concatenate([tab[1536:1664, :LANES], tab[1536:1664, LANES:]], axis=0)
    y = mm(tab[0:256, :], jnp.concatenate([high, low], axis=0)) + mm(ol, high)
    re, im = twist[:LANES, :], twist[LANES:, :]
    parts = []
    for s in (0, LANES):
        yr, yi = y[:LANES, s : s + LANES], y[LANES:, s : s + LANES]
        parts.append(jnp.concatenate([yr * re - yi * im, yr * im + yi * re], axis=1))
    high, low = split(jnp.concatenate(parts, axis=0))
    ih, il = tab[256:512, :], tab[512:768, :]
    return mm(high, ih) + mm(low, ih) + mm(high, il)


def conj_times(f, g):
    fr, fi, gr, gi = f[:, :LANES], f[:, LANES:], g[:, :LANES], g[:, LANES:]
    return jnp.concatenate([fr * gr + fi * gi, fr * gi - fi * gr], axis=1)


def backward(pa, pb, tab, twist):
    high, low = split(jnp.concatenate([pa, pb], axis=0))
    jh, jl = tab[768:1024, :], tab[1024:1280, :]
    v = mm(high, jh) + mm(low, jh) + mm(high, jl)
    re, im = twist[:LANES, :], twist[LANES:, :]
    parts = []
    for s in (0, LANES):
        vr, vi = v[s : s + LANES, :LANES], v[s : s + LANES, LANES:]
        parts.append(jnp.concatenate([vr * re + vi * im, vi * re - vr * im], axis=0))
    high, low = split(jnp.concatenate(parts, axis=1))
    bh, bl = tab[1280:1408, :], tab[1408:1536, :]
    return mm(bh, high) + mm(bh, low) + mm(bl, high)


def correlate(blocks, which, src, tab_in, twist_in, out, left, right, tab, twist, sems):
    pairs = (
        (src.at[:, pl.ds(8 * which, 8)], left),
        (src.at[:, pl.ds(8, 8)], right),
        (tab_in, tab),
        (twist_in, twist),
    )
    copies = [pltpu.make_async_copy(x, y, sems.at[i]) for i, (x, y) in enumerate(pairs)]
    for c in copies:
        c.start()
    for c in copies:
        c.wait()
    left, right = (x.reshape(32 * blocks, LANES) for x in (left, right))
    for ch in range(0, 8, 2):
        products = []
        for c in (ch, ch + 1):
            both = forward(load_pair(left, right, c, c, blocks), tab, twist)
            products.append(conj_times(both[:LANES], both[LANES:]))
        corr = backward(*products, tab, twist)
        for s in (0, 1):
            for i in range(4):
                out[pl.ds(i * 8 + ch + s, blocks, stride=32), :] = corr[
                    i * blocks : (i + 1) * blocks, s * LANES : (s + 1) * LANES
                ]


def first_kernel(blocks, src, tab, twist, ahead, out, *scratch):
    correlate(blocks, 0, src, tab, twist, out, *scratch)


def second_kernel(blocks, src, tab, twist, out, held, *scratch):
    correlate(blocks, 2, src, tab, twist, held, *scratch)
    for a in range(4 * blocks):
        out[:, a * LANES : (a + 1) * LANES] = held[a * 8 : (a + 1) * 8, :]


def put_ext(ext, i, prev, x):
    ext[i, 6:8, :] = prev[2 * i : 2 * i + 2, :]
    ext[i, 8:, :] = x[...]


def shorted(ext, i, taps, r0, n):
    return (
        taps[i, 0:1, :] * ext[i, 8 + r0 : 8 + r0 + n, :]
        + taps[i, 1:2, :] * ext[i, 7 + r0 : 7 + r0 + n, :]
        + taps[i, 2:3, :] * ext[i, 6 + r0 : 6 + r0 + n, :]
    )


def edge_kernel(q, k, v, go, cs, tails, heads):
    for i, x in enumerate((q, k, v)):
        tails[2 * i : 2 * i + 2, :] = x[6:8, :]
    tails[6:8, :] = jnp.zeros((2, q.shape[1]), f32)
    heads[...] = go[...] * cs[...]


def send_kernel(t_ref, taps, prev, q, k, v, go, fil, ahead, out, ext, gof, sems):
    n = q.shape[0]
    copies = [
        pltpu.make_async_copy(src, dst, sems.at[i])
        for i, (src, dst) in enumerate(
            (
                (fil, gof.at[0]),
                (k, ext.at[1, pl.ds(8, n)]),
                (v, ext.at[2, pl.ds(8, n)]),
                (q, ext.at[0, pl.ds(8, n)]),
                (go, gof.at[1]),
            )
        )
    ]
    for c in copies:
        c.start()
    t = t_ref[0]
    for i in range(3):
        ext[i, 6:8, :] = prev[2 * i : 2 * i + 2, :]
    groups = out.shape[0]
    owners = [owner_of(g, t) for g in range(groups)]

    def put(i, r0, piece):
        turned = jnp.transpose(piece)
        for g in range(groups):
            out[owners[g], r0 // LANES, i * 8 : i * 8 + 8, :] = turned[g * 8 : g * 8 + 8]

    starts = range(0, n, LANES)
    copies[0].wait()
    for r0 in starts:
        put(0, r0, gof[0, r0 : r0 + LANES, :])
    copies[1].wait()
    copies[2].wait()
    for r0 in starts:
        put(2, r0, shorted(ext, 1, taps, r0, LANES) * shorted(ext, 2, taps, r0, LANES))
    copies[3].wait()
    copies[4].wait()
    for r0 in starts:
        put(1, r0, gof[1, r0 : r0 + LANES, :] * shorted(ext, 0, taps, r0, LANES))


def side_kernel(
    taps, prev, q, k, v, go, cs, gain, following, zbase, ks, vs, gq, sums, ext, gext
):
    n = q.shape[0]
    for i, x in enumerate((q, k, v)):
        put_ext(ext, i, prev, x)
    gext[n : n + 8, :] = following[...]
    for r0 in range(0, n, LANES):
        gext[r0 : r0 + LANES, :] = go[r0 : r0 + LANES, :] * cs[r0 : r0 + LANES, :]
    totals = [jnp.zeros((1, q.shape[1]), f32) for _ in range(4)]
    for r0 in range(0, n, LANES):
        rows = slice(r0, r0 + LANES)
        gw = go[rows, :] * shorted(ext, 0, taps, r0, LANES)
        k_short = shorted(ext, 1, taps, r0, LANES)
        v_short = shorted(ext, 2, taps, r0, LANES)
        zbase[rows, :] = gain[...] * gw
        ks[rows, :] = k_short
        vs[rows, :] = v_short
        g = gext[rows, :]
        gq[rows, :] = (
            taps[0, 0:1, :] * g
            + taps[0, 1:2, :] * gext[r0 + 1 : r0 + 1 + LANES, :]
            + taps[0, 2:3, :] * gext[r0 + 2 : r0 + 2 + LANES, :]
        )
        for o in range(3):
            totals[o] += jnp.sum(
                g * ext[0, 8 + r0 - o : 8 + r0 - o + LANES, :], axis=0, keepdims=True
            )
        totals[3] += jnp.sum(gw * (k_short * v_short), axis=0, keepdims=True)
    for o in range(4):
        sums[o : o + 1, :] = totals[o]
    sums[4:, :] = jnp.zeros((4, q.shape[1]), f32)


def last_kernel(t_ref, corr, zbase, ks, vs, taps, prev, k, v, early, gk, gv, heads, sums, ext, gext, held):
    t = t_ref[0]
    n = k.shape[0]
    groups = corr.shape[0]
    owners = [owner_of(g, t) for g in range(groups)]
    for i, x in enumerate((k, v)):
        ext[i, 6:8, :] = prev[2 * i + 2 : 2 * i + 4, :]
        ext[i, 8:, :] = x[...]
        gext[i, n:, :] = jnp.zeros((8, k.shape[1]), f32)
    totals = [jnp.zeros((1, k.shape[1]), f32) for _ in range(6)]
    for r0 in range(0, n, LANES):
        rows = slice(r0, r0 + LANES)
        for g in range(groups):
            held[g * 8 : g * 8 + 8, :] = corr[owners[g], r0 // LANES]
        grad_z = zbase[rows, :] + jnp.transpose(held[...])
        for i, other in enumerate((vs, ks)):
            g = grad_z * other[rows, :]
            gext[i, rows, :] = g
            for o in range(3):
                totals[i * 3 + o] += jnp.sum(
                    g * ext[i, 8 + r0 - o : 8 + r0 - o + LANES, :], axis=0, keepdims=True
                )
    width = k.shape[1]
    totals = [early[o : o + 1, :] for o in range(4)] + totals
    for o in range(10):
        part = jnp.broadcast_to(totals[o].reshape(1, 1, width), (groups, 1, width))
        sums[:, :, o * width : (o + 1) * width] = part
    for i, out in enumerate((gk, gv)):
        heads[i] = gext[i, 0:2, :]
        for r0 in range(0, n, LANES):
            out[r0 : r0 + LANES, :] = (
                taps[i + 1, 0:1, :] * gext[i, r0 : r0 + LANES, :]
                + taps[i + 1, 1:2, :] * gext[i, r0 + 1 : r0 + 1 + LANES, :]
                + taps[i + 1, 2:3, :] * gext[i, r0 + 2 : r0 + 2 + LANES, :]
            )


def seam_kernel(gk_in, gv_in, nxt, taps, gk, gv):
    for i, (src, dst) in enumerate(((gk_in, gk), (gv_in, gv))):
        one, two = taps[i + 1, 1:2, :], taps[i + 1, 2:3, :]
        first, second = nxt[i, 0:1, :], nxt[i, 1:2, :]
        dst[...] = src[...]
        dst[6:7, :] = src[6:7, :] + two * first
        dst[7:8, :] = src[7:8, :] + one * first + two * second


def finish_kernel(parts, taps, skip):
    width = skip.shape[1]
    total = parts[0]
    for i in range(1, parts.shape[0]):
        total = total + parts[i]
    rows = [total[:, i * width : (i + 1) * width] for i in range(10)]
    skip[...] = rows.pop(3)
    for i in range(9):
        taps[i // 3, i % 3 : i % 3 + 1, :] = rows[i]


VM = pl.BlockSpec(memory_space=pltpu.VMEM)
SM = pl.BlockSpec(memory_space=pltpu.SMEM)
HB = pl.BlockSpec(memory_space=pl.ANY)


def shape(*s):
    return jax.ShapeDtypeStruct(s, f32)


def call(body, ins, outs, args, scratch=(), flops=10**6, nbytes=4 * 10**6):
    return pl.pallas_call(
        body,
        out_shape=outs,
        in_specs=ins,
        out_specs=jax.tree.map(lambda _: VM, outs),
        scratch_shapes=list(scratch),
        cost_estimate=pl.CostEstimate(flops=flops, bytes_accessed=nbytes, transcendentals=0),
        compiler_params=pltpu.CompilerParams(vmem_limit_bytes=40 * 2**20),
    )(*args)


def shifted(value, steps):
    count = lax.axis_size("ctx")
    pairs = [(i, i + steps) for i in range(count) if 0 <= i + steps < count]
    return lax.ppermute(value, "ctx", pairs)


def on_device(q, k, v, taps, fil, gain, cs, go):
    n, width = q.shape
    blocks = lax.axis_size("ctx")
    tp = lax.axis_size("tp")
    seq = n * blocks
    scale = 2.0 / (2 * seq) / math.sqrt(seq)
    tabs = [jnp.asarray(x) for x in tables(blocks, scale)]
    t = lax.axis_index("tp").astype(jnp.int32).reshape(1)

    low = pl.BlockSpec((8, width), lambda i: (n // 8 - 1, 0))
    top = pl.BlockSpec((8, width), lambda i: (0, 0))
    tails, heads = pl.pallas_call(
        edge_kernel,
        grid=(1,),
        out_shape=(shape(8, width), shape(8, width)),
        in_specs=[low, low, low, top, top],
        out_specs=(top, top),
        name="edge",
    )(q, k, v, go, cs)
    prev = shifted(tails, 1)
    nxt_q = shifted(heads, -1)

    ext3 = pltpu.VMEM((3, n + 8, width), f32)
    packed = call(
        send_kernel, [SM, VM, VM] + [HB] * 6, shape(blocks, n // LANES, 24, LANES),
        (t, taps, prev, q, k, v, go, fil, nxt_q),
        [ext3, pltpu.VMEM((2, n, width), f32), pltpu.SemaphoreType.DMA((5,))],
    )
    arrived = lax.all_to_all(packed, "ctx", 0, 0, tiled=True)
    arrived = arrived.reshape(seq // LANES, 24, LANES)
    work = [
        pltpu.VMEM((seq // LANES, 8, LANES), f32),
        pltpu.VMEM((seq // LANES, 8, LANES), f32),
        *(pltpu.VMEM(x.shape, x.dtype) for x in tabs),
        pltpu.SemaphoreType.DMA((4,)),
    ]
    zbase, ks, vs, gq, early = call(
        side_kernel, [VM] * 9,
        (shape(n, width),) * 4 + (shape(8, width),),
        (taps, prev, q, k, v, go, cs, gain.reshape(1, width), nxt_q),
        [ext3, pltpu.VMEM((n + 8, width), f32)],
    )
    corr = call(
        functools.partial(first_kernel, blocks), [HB] * 4,
        shape(seq * 8 // LANES, LANES), (arrived, *tabs, early), work,
        flops=2 * 10**9,
    )
    back = lax.all_to_all(corr.reshape(blocks, n // LANES, 8, LANES), "ctx", 0, 0, tiled=True)
    zeta = call(
        functools.partial(second_kernel, blocks), [HB] * 3,
        shape(8, seq), (arrived, *tabs),
        [pltpu.VMEM((seq * 8 // LANES, LANES), f32), *work], flops=2 * 10**9,
    )
    hop_one, hop_two = [], []
    for c in range(blocks):
        for s in range(tp):
            row, column = target_of(c, s)
            hop_one.append((c * tp + s, c * tp + column))
            hop_two.append((c * tp + column, row * tp + column))
    zeta = lax.ppermute(zeta, ("ctx", "tp"), hop_one)
    grad_filter = lax.ppermute(zeta, ("ctx", "tp"), hop_two)

    gk, gv, heads, parts = call(
        last_kernel, [SM] + [VM] * 9,
        (shape(n, width), shape(n, width), shape(2, 2, width), shape(blocks, 1, 10 * width)),
        (t, back, zbase, ks, vs, taps, prev, k, v, early),
        [
            pltpu.VMEM((2, n + 8, width), f32),
            pltpu.VMEM((2, n + 8, width), f32),
            pltpu.VMEM((width, LANES), f32),
        ],
    )
    parts = lax.all_to_all(parts, "ctx", 0, 0, tiled=True)
    nxt = shifted(heads, -1)
    gk, gv = pl.pallas_call(
        seam_kernel,
        grid=(1,),
        out_shape=(shape(n, width), shape(n, width)),
        in_specs=[low, low, VM, VM],
        out_specs=(low, low),
        input_output_aliases={0: 0, 1: 1},
        name="seam",
    )(gk, gv, nxt, taps)
    grad_taps, grad_skip = call(
        finish_kernel, [VM], (shape(3, 3, width), shape(1, width)), (parts,),
    )
    return gq, gk, gv, grad_filter, grad_taps, grad_skip.reshape(width)


def solution(mesh):
    rows = P("ctx", "tp")
    return jax.shard_map(
        on_device,
        mesh=mesh,
        in_specs=(rows, rows, rows, P(None, None, "tp"), rows, P("tp"), rows, rows),
        out_specs=(rows, rows, rows, P(("ctx", "tp"), None), P(None, None, "tp"), P("tp")),
        check_vma=False,
    )
```

profile of v0, /device:TPU:33, one launch (start us, length us, event | category | flops | bytes accessed | tf_op | source)
XLA Modules:
  0.0 125.9 jit_solution(10093976181202948169)
XLA Ops:
  0.6 0.0 copy-start.1
  0.6 0.0 copy-start
  0.7 0.0 copy-start.3
  0.7 0.0 copy-start.2
  0.7 0.0 copy-start.5
  0.7 1.5 %edge.1 = (f32[8,256]{1,0:T(8,128)}, f32[8,256]{1,0:T(8,128)}) custom-call(f32[512,256]{1,0:T(8,128)} %q.5, f32[512,256]{1,0:T(8,128)} %k.7, f32[512,256]{1,0:T(8,128)} %v.7, f32[512,256]{1,0:T(8,128)} %go.5, f32[512,256]{1,0:T(8,128)} %cs.3), custom_call_target="tpu_custom_call" | custom-call | tf_op jit(solution)/shard_map/edge/pallas_call | solution.py:346
  2.2 4.1 %collective-permute-start = (f32[8,256]{1,0:T(8,128)}, f32[8,256]{1,0:T(8,128)S(1)}, u32[]{:S(2)}, u32[]{:S(2)}) collective-permute-start(f32[8,256]{1,0:T(8,128)} %get-tuple-element.21), channel_id=1, source_target_pairs={{0,8},{8,16},{16,24},{24,32},{32,40},{40,48},{48,56},{56,64},{64,7... | collective-permute-start | bytes 24584 | tf_op jit(solution)/shard_map/ppermute | solution.py:332
  6.3 1.9 %collective-permute-start.1 = (f32[8,256]{1,0:T(8,128)}, f32[8,256]{1,0:T(8,128)S(1)}, u32[]{:S(2)}, u32[]{:S(2)}) collective-permute-start(f32[8,256]{1,0:T(8,128)} %get-tuple-element.22), channel_id=1, source_target_pairs={{8,0},{16,8},{24,16},{32,24},{40,32},{48,40},{56,48},{64,56},{72,6... | collective-permute-start | bytes 24584 | tf_op jit(solution)/shard_map/ppermute | solution.py:332
  8.2 0.0 collective-permute-done.prev
  8.2 3.2 %collective-permute-done.1.following.ahead = f32[8,256]{1,0:T(8,128)S(1)} collective-permute-done((f32[8,256]{1,0:T(8,128)}, f32[8,256]{1,0:T(8,128)S(1)}, u32[]{:S(2)}, u32[]{:S(2)}) %collective-permute-start.1) | collective-permute-done | bytes 8224 | tf_op jit(solution)/shard_map/ppermute | solution.py:332
  11.5 0.0 copy-done.1
  11.5 0.0 copy-done
  11.5 0.0 copy-done.3
  11.5 0.0 copy-done.2
  11.5 0.0 copy-done.5
  11.5 0.0 copy-start.10
  11.5 0.7 copy-done.10
  12.2 2.3 %shard_map.146 = f32[32,4,24,128]{3,2,1,0:T(8,128)} custom-call(s32[1]{0:T(128)} %bitcast.1.t_ref, f32[3,3,256]{2,1,0:T(4,128)S(1)} %copy-done.10, f32[8,256]{1,0:T(8,128)S(1)} %collective-permute-done.prev, f32[512,256]{1,0:T(8,128)S(1)} %copy-done.2, f32[512,256]{1,0:T(8,128)S(1)} %copy-done, f32[512,256]{1,0:T(8,128)S(1)} %copy-done.1, ...), custom_call_target="tpu_custom_call" | custom-call | flops 1000000 | bytes 4000000 | tf_op jit(solution)/shard_map/pallas_call | solution.py:318
  14.5 0.0 copy-start.4
  14.5 0.0 copy-start.11
  14.5 0.0 copy-start.12
  14.5 9.4 %all-to-all-start = ((f32[32,4,24,128]{3,2,1,0:T(8,128)}), f32[32,4,24,128]{3,2,1,0:T(8,128)}, u32[]{:S(2)}, u32[]{:S(2)}) async-start(f32[32,4,24,128]{3,2,1,0:T(8,128)} %shard_map.146), calls=%async_computation | async-start | bytes 3145728 | tf_op jit(solution)/shard_map/all_to_all | solution.py:363
  23.9 0.0 copy-start.15
  24.0 1.9 %shard_map.145 = (f32[512,256]{1,0:T(8,128)S(1)}, f32[512,256]{1,0:T(8,128)S(1)}, f32[512,256]{1,0:T(8,128)S(1)}, f32[512,256]{1,0:T(8,128)}, f32[8,256]{1,0:T(8,128)S(1)}) custom-call(f32[3,3,256]{2,1,0:T(4,128)S(1)} %copy-done.11, f32[8,256]{1,0:T(8,128)S(1)} %collective-permute-done.prev, f32[512,256]{1,0:T(8,128)S(1)} %copy-done.2, ...), custom_call_target="tpu_custom_call" | custom-call | flops 1000000 | bytes 4000000 | tf_op jit(solution)/shard_map/pallas_call | solution.py:318
  25.9 0.8 copy-done.6
  26.7 0.8 copy-done.8
  27.5 35.8 %all-to-all-done = f32[32,4,24,128]{3,2,1,0:T(8,128)} async-done(((f32[32,4,24,128]{3,2,1,0:T(8,128)}), f32[32,4,24,128]{3,2,1,0:T(8,128)}, u32[]{:S(2)}, u32[]{:S(2)}) %all-to-all-start) | async-done | bytes 1572896 | tf_op jit(solution)/shard_map/all_to_all | solution.py:363
  63.4 1.2 copy-done.13
  64.5 6.4 %shard_map.147 = f32[1024,128]{1,0:T(8,128)} custom-call(f32[128,24,128]{2,1,0:T(8,128)} %bitcast.2.src, bf16[1664,256]{1,0:T(8,128)(2,1)S(1)} %copy-done.13, f32[256,128]{1,0:T(8,128)S(1)} %copy-done.15, f32[8,256]{1,0:T(8,128)S(1)} %get-tuple-element.24.ahead.early), custom_call_target="tpu_custom_call" | custom-call | flops 2000000000 | bytes 4000000 | tf_op jit(solution)/shard_map/pallas_call | solution.py:318
  70.9 4.3 %all-to-all-start.1 = ((f32[32,4,8,128]{3,2,1,0:T(8,128)}), f32[32,4,8,128]{3,2,1,0:T(8,128)S(1)}, u32[]{:S(2)}, u32[]{:S(2)}) async-start(f32[32,4,8,128]{3,2,1,0:T(8,128)} %bitcast.3), calls=%async_computation.1 | async-start | bytes 1048576 | tf_op jit(solution)/shard_map/all_to_all | solution.py:382
  75.2 0.0 copy-start.14
  75.2 1.1 copy-done.14
  76.4 6.5 %shard_map.149 = f32[8,16384]{1,0:T(8,128)} custom-call(f32[128,24,128]{2,1,0:T(8,128)} %bitcast.2.src, bf16[1664,256]{1,0:T(8,128)(2,1)S(1)} %copy-done.14, f32[256,128]{1,0:T(8,128)S(1)} %copy-done.15), custom_call_target="tpu_custom_call" | custom-call | flops 2000000000 | bytes 4000000 | tf_op jit(solution)/shard_map/pallas_call | solution.py:318
  82.9 7.0 %collective-permute-start.3 = (f32[8,16384]{1,0:T(8,128)}, f32[8,16384]{1,0:T(8,128)}, u32[]{:S(2)}, u32[]{:S(2)}) collective-permute-start(f32[8,16384]{1,0:T(8,128)} %shard_map.149), channel_id=1, source_target_pairs={{0,0},{1,2},{2,1},{3,3},{4,4},{5,6},{6,5},{7,7},{8,13},{9,15},{10,... | collective-permute-start | bytes 1572872 | tf_op jit(solution)/shard_map/ppermute | solution.py:394
  89.9 1.7 %all-to-all-done.1.corr = f32[32,4,8,128]{3,2,1,0:T(8,128)S(1)} async-done(((f32[32,4,8,128]{3,2,1,0:T(8,128)}), f32[32,4,8,128]{3,2,1,0:T(8,128)S(1)}, u32[]{:S(2)}, u32[]{:S(2)}) %all-to-all-start.1) | async-done | bytes 524320 | tf_op jit(solution)/shard_map/all_to_all | solution.py:382
  91.6 0.0 copy-done.7
  91.6 2.0 %shard_map.148 = (f32[512,256]{1,0:T(8,128)}, f32[512,256]{1,0:T(8,128)}, f32[2,2,256]{2,1,0:T(2,128)S(1)}, f32[32,1,2560]{2,1,0:T(1,128)}) custom-call(s32[1]{0:T(128)} %bitcast.1.t_ref, f32[32,4,8,128]{3,2,1,0:T(8,128)S(1)} %all-to-all-done.1.corr, f32[512,256]{1,0:T(8,128)S(1)} %get-tuple-element.25.zbase, f32[512,256]{1,0:T(8,128)S(1)} %copy-done.7, ...), custom_call_target="tpu_custom_call" | custom-call | flops 1000000 | bytes 4000000 | tf_op jit(solution)/shard_map/pallas_call | solution.py:318
  93.6 6.3 %all-to-all-start.2 = ((f32[32,1,2560]{2,1,0:T(1,128)}), f32[32,1,2560]{2,1,0:T(1,128)S(1)}, u32[]{:S(2)}, u32[]{:S(2)}) async-start(f32[32,1,2560]{2,1,0:T(1,128)} %get-tuple-element.33), calls=%async_computation.2 | async-start | bytes 655360 | tf_op jit(solution)/shard_map/all_to_all | solution.py:407
  99.9 0.0 collective-permute-done.3
  100.0 7.0 %collective-permute-start.4 = (f32[8,16384]{1,0:T(8,128)}, f32[8,16384]{1,0:T(8,128)S(1)}, u32[]{:S(2)}, u32[]{:S(2)}) collective-permute-start(f32[8,16384]{1,0:T(8,128)} %collective-permute-done.3), channel_id=1, source_target_pairs={{0,0},{2,34},{1,81},{3,115},{4,132},{6,166},{5,213},{7,247},{13,13... | collective-permute-start | bytes 1572872 | tf_op jit(solution)/shard_map/ppermute | solution.py:395
  107.0 1.9 %collective-permute-start.2 = (f32[2,2,256]{2,1,0:T(2,128)S(1)}, f32[2,2,256]{2,1,0:T(2,128)S(1)}, u32[]{:S(2)}, u32[]{:S(2)}) collective-permute-start(f32[2,2,256]{2,1,0:T(2,128)S(1)} %get-tuple-element.30), channel_id=1, source_target_pairs={{8,0},{16,8},{24,16},{32,24},{40,32},{48,40},{56,48},{64,56},{72,6... | collective-permute-start | bytes 12296 | tf_op jit(solution)/shard_map/ppermute | solution.py:332
  108.9 3.3 %collective-permute-done.2.nxt = f32[2,2,256]{2,1,0:T(2,128)S(1)} collective-permute-done((f32[2,2,256]{2,1,0:T(2,128)S(1)}, f32[2,2,256]{2,1,0:T(2,128)S(1)}, u32[]{:S(2)}, u32[]{:S(2)}) %collective-permute-start.2) | collective-permute-done | bytes 4128 | tf_op jit(solution)/shard_map/ppermute | solution.py:332
  112.3 0.6 copy-done.16
  112.9 1.4 %seam.1 = (f32[512,256]{1,0:T(8,128)}, f32[512,256]{1,0:T(8,128)}) custom-call(f32[512,256]{1,0:T(8,128)} %get-tuple-element.28.gk_in, f32[512,256]{1,0:T(8,128)} %get-tuple-element.29.gv_in, f32[2,2,256]{2,1,0:T(2,128)} %copy-done.16, f32[3,3,256]{2,1,0:T(4,128)} %taps.7), custom_call_target="tpu_custom_call", output_to_operand_aliasing={{0}: (0, {}), {1}: (1, {})} | custom-call | tf_op jit(solution)/shard_map/seam/pallas_call | solution.py:409
  114.2 10.2 %collective-permute-done.4 = f32[8,16384]{1,0:T(8,128)S(1)} collective-permute-done((f32[8,16384]{1,0:T(8,128)}, f32[8,16384]{1,0:T(8,128)S(1)}, u32[]{:S(2)}, u32[]{:S(2)}) %collective-permute-start.4) | collective-permute-done | bytes 524320 | tf_op jit(solution)/shard_map/ppermute | solution.py:395
  124.4 0.0 all-to-all-done.2.parts
  124.4 0.6 shard_map.150
  125.1 0.8 copy.21
  (11 shorter events, 0.0 us)
Async XLA Ops:
  0.6 10.8 %copy-start.1 = (f32[512,256]{1,0:T(8,128)S(1)}, f32[512,256]{1,0:T(8,128)}, u32[]{:S(2)}) copy-start(f32[512,256]{1,0:T(8,128)} %v.7) | copy-start | bytes 1572868
  0.6 10.8 %copy-start = (f32[512,256]{1,0:T(8,128)S(1)}, f32[512,256]{1,0:T(8,128)}, u32[]{:S(2)}) copy-start(f32[512,256]{1,0:T(8,128)} %k.7) | copy-start | bytes 1572868
  0.7 10.8 %copy-start.3 = (f32[512,256]{1,0:T(8,128)S(1)}, f32[512,256]{1,0:T(8,128)}, u32[]{:S(2)}) copy-start(f32[512,256]{1,0:T(8,128)} %go.5) | copy-start | bytes 1572868
  0.7 10.8 %copy-start.2 = (f32[512,256]{1,0:T(8,128)S(1)}, f32[512,256]{1,0:T(8,128)}, u32[]{:S(2)}) copy-start(f32[512,256]{1,0:T(8,128)} %q.5) | copy-start | bytes 1572868
  0.7 10.8 %copy-start.5 = (f32[512,256]{1,0:T(8,128)S(1)}, f32[512,256]{1,0:T(8,128)}, u32[]{:S(2)}) copy-start(f32[512,256]{1,0:T(8,128)} %fil.1) | copy-start | bytes 1572868
  2.2 6.0 %collective-permute-start = (f32[8,256]{1,0:T(8,128)}, f32[8,256]{1,0:T(8,128)S(1)}, u32[]{:S(2)}, u32[]{:S(2)}) collective-permute-start(f32[8,256]{1,0:T(8,128)} %get-tuple-element.21), channel_id=1, source_target_pairs={{0,8},{8,16},{16,24},{24,32},{32,40},{40,48},{48,56},{56,64},{64,7... | collective-permute-start | bytes 24584 | tf_op jit(solution)/shard_map/ppermute | solution.py:332
  6.3 5.2 %collective-permute-start.1 = (f32[8,256]{1,0:T(8,128)}, f32[8,256]{1,0:T(8,128)S(1)}, u32[]{:S(2)}, u32[]{:S(2)}) collective-permute-start(f32[8,256]{1,0:T(8,128)} %get-tuple-element.22), channel_id=1, source_target_pairs={{8,0},{16,8},{24,16},{32,24},{40,32},{48,40},{56,48},{64,56},{72,6... | collective-permute-start | bytes 24584 | tf_op jit(solution)/shard_map/ppermute | solution.py:332
  11.5 0.7 copy-start.10
  14.5 9.5 %copy-start.4 = (f32[512,256]{1,0:T(8,128)S(1)}, f32[512,256]{1,0:T(8,128)}, u32[]{:S(2)}) copy-start(f32[512,256]{1,0:T(8,128)} %cs.3) | copy-start | bytes 1572868
  14.5 9.5 %copy-start.11 = (f32[3,3,256]{2,1,0:T(4,128)S(1)}, f32[3,3,256]{2,1,0:T(4,128)}, u32[]{:S(2)}) copy-start(f32[3,3,256]{2,1,0:T(4,128)} %taps.7) | copy-start | bytes 27652
  14.5 9.5 %copy-start.12 = (f32[256]{0:T(256)S(1)}, f32[256]{0:T(256)}, u32[]{:S(2)}) copy-start(f32[256]{0:T(256)} %param.15) | copy-start | bytes 3076
  14.5 48.8 %all-to-all-start = ((f32[32,4,24,128]{3,2,1,0:T(8,128)}), f32[32,4,24,128]{3,2,1,0:T(8,128)}, u32[]{:S(2)}, u32[]{:S(2)}) async-start(f32[32,4,24,128]{3,2,1,0:T(8,128)} %shard_map.146), calls=%async_computation | async-start | bytes 3145728 | tf_op jit(solution)/shard_map/all_to_all | solution.py:363
  23.9 39.4 %copy-start.15 = (f32[256,128]{1,0:T(8,128)S(1)}, f32[256,128]{1,0:T(8,128)}, u32[]{:S(2)}) copy-start(f32[256,128]{1,0:T(8,128)} %constant.9.clone.twist) | copy-start | bytes 393220
  25.9 0.8 copy-start.6
  26.7 0.8 copy-start.8
  63.4 1.2 copy-start.13
  70.9 20.7 %all-to-all-start.1 = ((f32[32,4,8,128]{3,2,1,0:T(8,128)}), f32[32,4,8,128]{3,2,1,0:T(8,128)S(1)}, u32[]{:S(2)}, u32[]{:S(2)}) async-start(f32[32,4,8,128]{3,2,1,0:T(8,128)} %bitcast.3), calls=%async_computation.1 | async-start | bytes 1048576 | tf_op jit(solution)/shard_map/all_to_all | solution.py:382
  75.2 1.2 copy-start.14
  76.4 15.2 %copy-start.7 = (f32[512,256]{1,0:T(8,128)S(1)}, f32[512,256]{1,0:T(8,128)}, u32[]{:S(2)}) copy-start(f32[512,256]{1,0:T(8,128)} %copy-done.6) | copy-start | bytes 1572868
  76.4 15.2 %copy-start.9 = (f32[512,256]{1,0:T(8,128)S(1)}, f32[512,256]{1,0:T(8,128)}, u32[]{:S(2)}) copy-start(f32[512,256]{1,0:T(8,128)} %copy-done.8) | copy-start | bytes 1572868
  82.9 17.0 %collective-permute-start.3 = (f32[8,16384]{1,0:T(8,128)}, f32[8,16384]{1,0:T(8,128)}, u32[]{:S(2)}, u32[]{:S(2)}) collective-permute-start(f32[8,16384]{1,0:T(8,128)} %shard_map.149), channel_id=1, source_target_pairs={{0,0},{1,2},{2,1},{3,3},{4,4},{5,6},{6,5},{7,7},{8,13},{9,15},{10,... | collective-permute-start | bytes 1572872 | tf_op jit(solution)/shard_map/ppermute | solution.py:394
  93.6 30.8 %all-to-all-start.2 = ((f32[32,1,2560]{2,1,0:T(1,128)}), f32[32,1,2560]{2,1,0:T(1,128)S(1)}, u32[]{:S(2)}, u32[]{:S(2)}) async-start(f32[32,1,2560]{2,1,0:T(1,128)} %get-tuple-element.33), calls=%async_computation.2 | async-start | bytes 655360 | tf_op jit(solution)/shard_map/all_to_all | solution.py:407
  100.0 24.5 %collective-permute-start.4 = (f32[8,16384]{1,0:T(8,128)}, f32[8,16384]{1,0:T(8,128)S(1)}, u32[]{:S(2)}, u32[]{:S(2)}) collective-permute-start(f32[8,16384]{1,0:T(8,128)} %collective-permute-done.3), channel_id=1, source_target_pairs={{0,0},{2,34},{1,81},{3,115},{4,132},{6,166},{5,213},{7,247},{13,13... | collective-permute-start | bytes 1572872 | tf_op jit(solution)/shard_map/ppermute | solution.py:395
  107.0 5.3 %collective-permute-start.2 = (f32[2,2,256]{2,1,0:T(2,128)S(1)}, f32[2,2,256]{2,1,0:T(2,128)S(1)}, u32[]{:S(2)}, u32[]{:S(2)}) collective-permute-start(f32[2,2,256]{2,1,0:T(2,128)S(1)} %get-tuple-element.30), channel_id=1, source_target_pairs={{8,0},{16,8},{24,16},{32,24},{40,32},{48,40},{56,48},{64,56},{72,6... | collective-permute-start | bytes 12296 | tf_op jit(solution)/shard_map/ppermute | solution.py:332
  112.3 0.6 copy-start.16
where the time goes:
time: 127 us; the launch traced here: 126 us
  waiting for transfers between devices  54.3 us (43%)
  starting transfers between devices  42 us (33%)
  Pallas kernels  22.6 us (18%)
  local copies, waits for them, and re-layouts  6.03 us (5%)
    all_to_all x1, waiting for transfers between devices, on_device(): arrived = lax.all_to_all(packed, 'ctx', 0, 0, tiled=True)  35.8 us
    pallas_call x6, Pallas kernels, call(): pl.pallas_call(body, out_shape=outs, in_specs=ins, out_specs=jax.tree.map...  19.7 us
    ppermute x1, waiting for transfers between devices, on_device(): grad_filter = lax.ppermute(zeta, ('ctx', 'tp'), hop_two)  10.2 us
    all_to_all x1, starting transfers between devices, on_device(): arrived = lax.all_to_all(packed, 'ctx', 0, 0, tiled=True)  9.42 us
    ppermute x3, starting transfers between devices, shifted(): return lax.ppermute(value, 'ctx', pairs)  7.93 us
    ppermute x1, starting transfers between devices, on_device(): grad_filter = lax.ppermute(zeta, ('ctx', 'tp'), hop_two)  7.05 us
    ppermute x1, starting transfers between devices, on_device(): zeta = lax.ppermute(zeta, ('ctx', 'tp'), hop_one)  6.99 us
    ppermute x3, waiting for transfers between devices, shifted(): return lax.ppermute(value, 'ctx', pairs)  6.58 us
  transfers between devices with their start and end apart: 8, of which 5 were waited for; matrix products, arithmetic and copies ran while one was open for 0% of the time, Pallas kernels for 9%

commit v1 on v0

--- a/solution.py
+++ b/solution.py
@@ -147,10 +147,12 @@
     correlate(blocks, 0, src, tab, twist, out, *scratch)
 
 
-def second_kernel(blocks, src, tab, twist, out, held, *scratch):
+def second_kernel(blocks, src, tab, twist, early, late, held, *scratch):
     correlate(blocks, 2, src, tab, twist, held, *scratch)
-    for a in range(4 * blocks):
-        out[:, a * LANES : (a + 1) * LANES] = held[a * 8 : (a + 1) * 8, :]
+    half = 2 * blocks
+    for a in range(half):
+        early[:, a * LANES : (a + 1) * LANES] = held[a * 8 : (a + 1) * 8, :]
+        late[:, a * LANES : (a + 1) * LANES] = held[(half + a) * 8 : (half + a + 1) * 8, :]
 
 
 def put_ext(ext, i, prev, x):
@@ -173,7 +175,7 @@
     heads[...] = go[...] * cs[...]
 
 
-def send_kernel(t_ref, taps, prev, q, k, v, go, fil, ahead, out, ext, gof, sems):
+def send_kernel(t_ref, taps, prev, q, k, v, go, fil, out, ext, gof, sems):
     n = q.shape[0]
     copies = [
         pltpu.make_async_copy(src, dst, sems.at[i])
@@ -248,7 +250,9 @@
     sums[4:, :] = jnp.zeros((4, q.shape[1]), f32)
 
 
-def last_kernel(t_ref, corr, zbase, ks, vs, taps, prev, k, v, early, gk, gv, heads, sums, ext, gext, held):
+def last_kernel(
+    t_ref, corr, zbase, ks, vs, taps, prev, k, v, early, gk, gv, heads, keep, give, ext, gext, held
+):
     t = t_ref[0]
     n = k.shape[0]
     groups = corr.shape[0]
@@ -272,9 +276,12 @@
                 )
     width = k.shape[1]
     totals = [early[o : o + 1, :] for o in range(4)] + totals
-    for o in range(10):
-        part = jnp.broadcast_to(totals[o].reshape(1, 1, width), (groups, 1, width))
-        sums[:, :, o * width : (o + 1) * width] = part
+    even = t_ref[1] == 0
+    for o in range(5):
+        keep[o : o + 1, :] = jnp.where(even, totals[o], totals[5 + o])
+        give[o : o + 1, :] = jnp.where(even, totals[5 + o], totals[o])
+    for x in (keep, give):
+        x[5:8, :] = jnp.zeros((3, width), f32)
     for i, out in enumerate((gk, gv)):
         heads[i] = gext[i, 0:2, :]
         for r0 in range(0, n, LANES):
@@ -294,12 +301,28 @@
         dst[7:8, :] = src[7:8, :] + one * first + two * second
 
 
-def finish_kernel(parts, taps, skip):
-    width = skip.shape[1]
+def spread_kernel(mine, got, out):
+    width = mine.shape[1]
+    both = mine[...] + got[...]
+    for o in range(5):
+        part = both[o : o + 1, :].reshape(1, 1, width)
+        out[:, :, o * width : (o + 1) * width] = jnp.broadcast_to(part, (out.shape[0], 1, width))
+
+
+def gather_kernel(parts, out):
+    width = out.shape[1]
     total = parts[0]
     for i in range(1, parts.shape[0]):
         total = total + parts[i]
-    rows = [total[:, i * width : (i + 1) * width] for i in range(10)]
+    for o in range(5):
+        out[o : o + 1, :] = total[:, o * width : (o + 1) * width]
+    out[5:8, :] = jnp.zeros((3, width), f32)
+
+
+def finish_kernel(t_ref, mine, other, taps, skip):
+    even = t_ref[1] == 0
+    rows = [jnp.where(even, mine[o : o + 1, :], other[o : o + 1, :]) for o in range(5)]
+    rows += [jnp.where(even, other[o : o + 1, :], mine[o : o + 1, :]) for o in range(5)]
     skip[...] = rows.pop(3)
     for i in range(9):
         taps[i // 3, i % 3 : i % 3 + 1, :] = rows[i]
@@ -308,6 +331,7 @@
 VM = pl.BlockSpec(memory_space=pltpu.VMEM)
 SM = pl.BlockSpec(memory_space=pltpu.SMEM)
 HB = pl.BlockSpec(memory_space=pl.ANY)
+TB = pl.BlockSpec(memory_space=pltpu.HBM)
 
 
 def shape(*s):
@@ -339,7 +363,8 @@
     seq = n * blocks
     scale = 2.0 / (2 * seq) / math.sqrt(seq)
     tabs = [jnp.asarray(x) for x in tables(blocks, scale)]
-    t = lax.axis_index("tp").astype(jnp.int32).reshape(1)
+    where = [lax.axis_index("tp"), lax.axis_index("ctx") & 1]
+    t = jnp.stack([x.astype(jnp.int32) for x in where])
 
     low = pl.BlockSpec((8, width), lambda i: (n // 8 - 1, 0))
     top = pl.BlockSpec((8, width), lambda i: (0, 0))
@@ -356,8 +381,8 @@
 
     ext3 = pltpu.VMEM((3, n + 8, width), f32)
     packed = call(
-        send_kernel, [SM, VM, VM] + [HB] * 6, shape(blocks, n // LANES, 24, LANES),
-        (t, taps, prev, q, k, v, go, fil, nxt_q),
+        send_kernel, [SM, VM, VM] + [HB] * 5, shape(blocks, n // LANES, 24, LANES),
+        (t, taps, prev, q, k, v, go, fil),
         [ext3, pltpu.VMEM((2, n, width), f32), pltpu.SemaphoreType.DMA((5,))],
     )
     arrived = lax.all_to_all(packed, "ctx", 0, 0, tiled=True)
@@ -375,14 +400,14 @@
         [ext3, pltpu.VMEM((n + 8, width), f32)],
     )
     corr = call(
-        functools.partial(first_kernel, blocks), [HB] * 4,
+        functools.partial(first_kernel, blocks), [HB, TB, TB, HB],
         shape(seq * 8 // LANES, LANES), (arrived, *tabs, early), work,
         flops=2 * 10**9,
     )
     back = lax.all_to_all(corr.reshape(blocks, n // LANES, 8, LANES), "ctx", 0, 0, tiled=True)
     zeta = call(
-        functools.partial(second_kernel, blocks), [HB] * 3,
-        shape(8, seq), (arrived, *tabs),
+        functools.partial(second_kernel, blocks), [HB, TB, TB],
+        (shape(8, seq // 2), shape(8, seq // 2)), (arrived, *tabs),
         [pltpu.VMEM((seq * 8 // LANES, LANES), f32), *work], flops=2 * 10**9,
     )
     hop_one, hop_two = [], []
@@ -391,12 +416,14 @@
             row, column = target_of(c, s)
             hop_one.append((c * tp + s, c * tp + column))
             hop_two.append((c * tp + column, row * tp + column))
-    zeta = lax.ppermute(zeta, ("ctx", "tp"), hop_one)
-    grad_filter = lax.ppermute(zeta, ("ctx", "tp"), hop_two)
-
-    gk, gv, heads, parts = call(
+    zeta = [lax.ppermute(x, ("ctx", "tp"), hop_one) for x in zeta]
+    early_half = lax.ppermute(zeta[0], ("ctx", "tp"), hop_two)
+    late_half = lax.ppermute(zeta[1], ("ctx", "tp"), hop_two)
+    grad_filter = jnp.concatenate([early_half, late_half], axis=1)
+
+    gk, gv, heads, keep, give = call(
         last_kernel, [SM] + [VM] * 9,
-        (shape(n, width), shape(n, width), shape(2, 2, width), shape(blocks, 1, 10 * width)),
+        (shape(n, width), shape(n, width), shape(2, 2, width), shape(8, width), shape(8, width)),
         (t, back, zbase, ks, vs, taps, prev, k, v, early),
         [
             pltpu.VMEM((2, n + 8, width), f32),
@@ -404,7 +431,15 @@
             pltpu.VMEM((width, LANES), f32),
         ],
     )
-    parts = lax.all_to_all(parts, "ctx", 0, 0, tiled=True)
+    swap = [(i, i ^ 1) for i in range(blocks)]
+    got = lax.ppermute(give, "ctx", swap)
+    parts = call(spread_kernel, [VM, VM], shape(blocks // 2, 1, 5 * width), (keep, got))
+    same = [list(range(core, blocks, 2)) for core in (0, 1)]
+    parts = lax.all_to_all(
+        parts, "ctx", 0, 0, axis_index_groups=same, tiled=True
+    )
+    total = call(gather_kernel, [VM], shape(8, width), (parts,))
+    other = lax.ppermute(total, "ctx", swap)
     nxt = shifted(heads, -1)
     gk, gv = pl.pallas_call(
         seam_kernel,
@@ -416,7 +451,7 @@
         name="seam",
     )(gk, gv, nxt, taps)
     grad_taps, grad_skip = call(
-        finish_kernel, [VM], (shape(3, 3, width), shape(1, width)), (parts,),
+        finish_kernel, [SM, VM, VM], (shape(3, 3, width), shape(1, width)), (t, total, other),
     )
     return gq, gk, gv, grad_filter, grad_taps, grad_skip.reshape(width)
 

time: 127 us -> 133 us (1.047)
  the two profiles are of different devices: /device:TPU:33 before, /device:TPU:1 now
where the time goes in v1:
time: 133 us; the launch traced here: 131 us
  starting transfers between devices  54 us (41%)
  waiting for transfers between devices  45.7 us (34%)
  Pallas kernels  24 us (18%)
  local copies, waits for them, and re-layouts  4.55 us (3%)
  other arithmetic  1.85 us (1%)
    ppermute x3, waiting for transfers between devices, shifted(): return lax.ppermute(value, 'ctx', pairs)  35.1 us
    pallas_call x8, Pallas kernels, call(): pl.pallas_call(body, out_shape=outs, in_specs=ins, out_specs=jax.tree.map...  21.1 us
    all_to_all x1, starting transfers between devices, on_device(): arrived = lax.all_to_all(packed, 'ctx', 0, 0, tiled=True)  11.7 us
    ppermute x3, starting transfers between devices, shifted(): return lax.ppermute(value, 'ctx', pairs)  9.61 us
    ppermute x2, starting transfers between devices, on_device(): zeta = [lax.ppermute(x, ('ctx', 'tp'), hop_one) for x in zeta]  9.07 us
    all_to_all x1, starting transfers between devices, on_device(): lax.all_to_all(parts, 'ctx', 0, 0, axis_index_groups=same, tiled=True)  8.85 us
    all_to_all x1, starting transfers between devices, on_device(): lax.all_to_all(corr.reshape(blocks, n // LANES, 8, LANES), 'ctx', 0, 0, t...  6.79 us
    all_to_all x1, waiting for transfers between devices, on_device(): lax.all_to_all(parts, 'ctx', 0, 0, axis_index_groups=same, tiled=True)  5.02 us
  transfers between devices with their start and end apart: 12, of which 6 were waited for; matrix products, arithmetic and copies ran while one was open for 1% of the time, Pallas kernels for 9%

profile of v1, /device:TPU:1, one launch (start us, length us, event | category | flops | bytes accessed | tf_op | source)
XLA Modules:
  0.0 131.0 jit_solution(15987393383509961097)
XLA Ops:
  0.7 0.0 copy-start.10
  0.7 0.0 copy-start.5
  0.7 1.5 %edge.1 = (f32[8,256]{1,0:T(8,128)}, f32[8,256]{1,0:T(8,128)}) custom-call(f32[512,256]{1,0:T(8,128)} %q.5, f32[512,256]{1,0:T(8,128)} %k.7, f32[512,256]{1,0:T(8,128)} %v.7, f32[512,256]{1,0:T(8,128)} %go.5, f32[512,256]{1,0:T(8,128)} %cs.3), custom_call_target="tpu_custom_call" | custom-call | tf_op jit(solution)/shard_map/edge/pallas_call | solution.py:371
  2.2 4.9 %collective-permute-start = (f32[8,256]{1,0:T(8,128)}, f32[8,256]{1,0:T(8,128)S(1)}, u32[]{:S(2)}, u32[]{:S(2)}) collective-permute-start(f32[8,256]{1,0:T(8,128)} %get-tuple-element.24), channel_id=1, source_target_pairs={{0,8},{8,16},{16,24},{24,32},{32,40},{40,48},{48,56},{56,64},{64,7... | collective-permute-start | bytes 24584 | tf_op jit(solution)/shard_map/ppermute | solution.py:356
  7.1 0.1 pad_add_fusion.t_ref
  7.2 0.9 collective-permute-done.prev
  8.1 0.0 copy-done.3
  8.1 2.8 %shard_map.146 = f32[32,4,24,128]{3,2,1,0:T(8,128)} custom-call(s32[2]{0:T(128)S(1)} %pad_add_fusion.t_ref, f32[3,3,256]{2,1,0:T(4,128)S(1)} %copy-done.10, f32[8,256]{1,0:T(8,128)S(1)} %collective-permute-done.prev, f32[512,256]{1,0:T(8,128)S(1)} %copy-done.2, f32[512,256]{1,0:T(8,128)S(1)} %copy-done, f32[512,256]{1,0:T(8,128)S(1)} %copy-done.1, ...), custom_call_target="tpu_custom_call" | custom-call | flops 1000000 | bytes 4000000 | tf_op jit(solution)/shard_map/pallas_call | solution.py:342
  10.9 0.0 copy-start.16
  11.0 0.0 copy-start.4
  11.0 0.0 copy-start.11
  11.0 11.7 %all-to-all-start = ((f32[32,4,24,128]{3,2,1,0:T(8,128)}), f32[32,4,24,128]{3,2,1,0:T(8,128)}, u32[]{:S(2)}, u32[]{:S(2)}) async-start(f32[32,4,24,128]{3,2,1,0:T(8,128)} %shard_map.146), calls=%async_computation | async-start | bytes 3145728 | tf_op jit(solution)/shard_map/all_to_all | solution.py:388
  22.7 0.0 copy-start.14
  22.7 2.3 %collective-permute-start.1 = (f32[8,256]{1,0:T(8,128)S(1)}, f32[8,256]{1,0:T(8,128)S(1)}, u32[]{:S(2)}, u32[]{:S(2)}) collective-permute-start(f32[8,256]{1,0:T(8,128)S(1)} %copy-done.16), channel_id=1, source_target_pairs={{8,0},{16,8},{24,16},{32,24},{40,32},{48,40},{56,48},{64,56},{72,6... | collective-permute-start | bytes 24584 | tf_op jit(solution)/shard_map/ppermute | solution.py:356
  25.1 34.2 %collective-permute-done.1.following = f32[8,256]{1,0:T(8,128)S(1)} collective-permute-done((f32[8,256]{1,0:T(8,128)S(1)}, f32[8,256]{1,0:T(8,128)S(1)}, u32[]{:S(2)}, u32[]{:S(2)}) %collective-permute-start.1) | collective-permute-done | bytes 8224 | tf_op jit(solution)/shard_map/ppermute | solution.py:356
  59.3 1.9 %shard_map.145 = (f32[512,256]{1,0:T(8,128)S(1)}, f32[512,256]{1,0:T(8,128)S(1)}, f32[512,256]{1,0:T(8,128)S(1)}, f32[512,256]{1,0:T(8,128)}, f32[8,256]{1,0:T(8,128)S(1)}) custom-call(f32[3,3,256]{2,1,0:T(4,128)S(1)} %copy-done.10, f32[8,256]{1,0:T(8,128)S(1)} %collective-permute-done.prev, f32[512,256]{1,0:T(8,128)S(1)} %copy-done.2, ...), custom_call_target="tpu_custom_call" | custom-call | flops 1000000 | bytes 4000000 | tf_op jit(solution)/shard_map/pallas_call | solution.py:342
  61.2 0.8 copy-done.6
  62.0 0.8 copy-done.8
  62.8 0.0 all-to-all-done
  62.8 1.2 copy-done.12
  63.9 6.4 %shard_map.147 = f32[1024,128]{1,0:T(8,128)} custom-call(f32[128,24,128]{2,1,0:T(8,128)} %bitcast.3.src, bf16[1664,256]{1,0:T(8,128)(2,1)S(1)} %copy-done.12, f32[256,128]{1,0:T(8,128)S(1)} %copy-done.14, f32[8,256]{1,0:T(8,128)S(1)} %get-tuple-element.27.ahead.early), custom_call_target="tpu_custom_call" | custom-call | flops 2000000000 | bytes 4000000 | tf_op jit(solution)/shard_map/pallas_call | solution.py:342
  70.3 6.8 %all-to-all-start.1 = ((f32[32,4,8,128]{3,2,1,0:T(8,128)}), f32[32,4,8,128]{3,2,1,0:T(8,128)S(1)}, u32[]{:S(2)}, u32[]{:S(2)}) async-start(f32[32,4,8,128]{3,2,1,0:T(8,128)} %bitcast.4), calls=%async_computation.1 | async-start | bytes 1048576 | tf_op jit(solution)/shard_map/all_to_all | solution.py:407
  77.1 0.0 copy-start.13
  77.1 1.1 copy-done.13
  78.3 5.7 %shard_map.149 = (f32[8,8192]{1,0:T(8,128)S(1)}, f32[8,8192]{1,0:T(8,128)S(1)}) custom-call(f32[128,24,128]{2,1,0:T(8,128)} %bitcast.3.src, bf16[1664,256]{1,0:T(8,128)(2,1)S(1)} %copy-done.13, f32[256,128]{1,0:T(8,128)S(1)} %copy-done.14), custom_call_target="tpu_custom_call" | custom-call | flops 2000000000 | bytes 4000000 | tf_op jit(solution)/shard_map/pallas_call | solution.py:342
  84.0 7.0 %collective-permute-start.3 = (f32[8,8192]{1,0:T(8,128)S(1)}, f32[8,8192]{1,0:T(8,128)}, u32[]{:S(2)}, u32[]{:S(2)}) collective-permute-start(f32[8,8192]{1,0:T(8,128)S(1)} %get-tuple-element.36), channel_id=1, source_target_pairs={{0,0},{1,2},{2,1},{3,3},{4,4},{5,6},{6,5},{7,7},{8,13},{9,15},{10,... | collective-permute-start | bytes 786440 | tf_op jit(solution)/shard_map/ppermute | solution.py:419
  91.0 2.1 %collective-permute-start.5 = (f32[8,8192]{1,0:T(8,128)S(1)}, f32[8,8192]{1,0:T(8,128)}, u32[]{:S(2)}, u32[]{:S(2)}) collective-permute-start(f32[8,8192]{1,0:T(8,128)S(1)} %get-tuple-element.37), channel_id=1, source_target_pairs={{0,0},{1,2},{2,1},{3,3},{4,4},{5,6},{6,5},{7,7},{8,13},{9,15},{10,... | collective-permute-start | bytes 786440 | tf_op jit(solution)/shard_map/ppermute | solution.py:419
  93.1 1.6 %collective-permute-done.3 = f32[8,8192]{1,0:T(8,128)} collective-permute-done((f32[8,8192]{1,0:T(8,128)S(1)}, f32[8,8192]{1,0:T(8,128)}, u32[]{:S(2)}, u32[]{:S(2)}) %collective-permute-start.3) | collective-permute-done | bytes 262176 | tf_op jit(solution)/shard_map/ppermute | solution.py:419
  94.7 1.9 %collective-permute-start.4 = (f32[8,8192]{1,0:T(8,128)}, f32[8,8192]{1,0:T(8,128)S(1)}, u32[]{:S(2)}, u32[]{:S(2)}) collective-permute-start(f32[8,8192]{1,0:T(8,128)} %collective-permute-done.3), channel_id=1, source_target_pairs={{0,0},{2,34},{1,81},{3,115},{4,132},{6,166},{5,213},{7,247},{13,13... | collective-permute-start | bytes 786440 | tf_op jit(solution)/shard_map/ppermute | solution.py:420
  96.6 2.9 %collective-permute-done.5 = f32[8,8192]{1,0:T(8,128)} collective-permute-done((f32[8,8192]{1,0:T(8,128)S(1)}, f32[8,8192]{1,0:T(8,128)}, u32[]{:S(2)}, u32[]{:S(2)}) %collective-permute-start.5) | collective-permute-done | bytes 262176 | tf_op jit(solution)/shard_map/ppermute | solution.py:419
  99.4 4.4 %collective-permute-start.6 = (f32[8,8192]{1,0:T(8,128)}, f32[8,8192]{1,0:T(8,128)}, u32[]{:S(2)}, u32[]{:S(2)}) collective-permute-start(f32[8,8192]{1,0:T(8,128)} %collective-permute-done.5), channel_id=1, source_target_pairs={{0,0},{2,34},{1,81},{3,115},{4,132},{6,166},{5,213},{7,247},{13,13... | collective-permute-start | bytes 786440 | tf_op jit(solution)/shard_map/ppermute | solution.py:421
  103.9 0.0 all-to-all-done.1.corr
  103.9 2.4 %shard_map.148 = (f32[512,256]{1,0:T(8,128)}, f32[512,256]{1,0:T(8,128)}, f32[2,2,256]{2,1,0:T(2,128)S(1)}, f32[8,256]{1,0:T(8,128)S(1)}, f32[8,256]{1,0:T(8,128)S(1)}) custom-call(s32[2]{0:T(128)S(1)} %pad_add_fusion.t_ref, f32[32,4,8,128]{3,2,1,0:T(8,128)S(1)} %all-to-all-done.1.corr, f32[512,256]{1,0:T(8,128)S(1)} %get-tuple-element.28.zbase, ...), custom_call_target="tpu_custom_call" | custom-call | flops 1000000 | bytes 4000000 | tf_op jit(solution)/shard_map/pallas_call | solution.py:342
  106.3 0.0 collective-permute-start.7
  106.3 1.2 collective-permute-done.7.got
  107.5 0.7 shard_map.150
  108.2 8.8 %all-to-all-start.2 = ((f32[16,1,1280]{2,1,0:T(1,128)}), f32[16,1,1280]{2,1,0:T(1,128)S(1)}, u32[]{:S(2)}, u32[]{:S(2)}) async-start(f32[16,1,1280]{2,1,0:T(1,128)} %shard_map.150), calls=%async_computation.2 | async-start | bytes 163840 | tf_op jit(solution)/shard_map/all_to_all | solution.py:438
  117.0 2.4 %collective-permute-start.2 = (f32[2,2,256]{2,1,0:T(2,128)S(1)}, f32[2,2,256]{2,1,0:T(2,128)S(1)}, u32[]{:S(2)}, u32[]{:S(2)}) collective-permute-start(f32[2,2,256]{2,1,0:T(2,128)S(1)} %get-tuple-element.33), channel_id=1, source_target_pairs={{8,0},{16,8},{24,16},{32,24},{40,32},{48,40},{56,48},{64,56},{72,6... | collective-permute-start | bytes 12296 | tf_op jit(solution)/shard_map/ppermute | solution.py:356
  119.4 5.0 %all-to-all-done.2.parts = f32[16,1,1280]{2,1,0:T(1,128)S(1)} async-done(((f32[16,1,1280]{2,1,0:T(1,128)}), f32[16,1,1280]{2,1,0:T(1,128)S(1)}, u32[]{:S(2)}, u32[]{:S(2)}) %all-to-all-start.2) | async-done | bytes 81952 | tf_op jit(solution)/shard_map/all_to_all | solution.py:438
  124.4 1.7 %collective-permute-start.8 = (f32[8,256]{1,0:T(8,128)S(1)}, f32[8,256]{1,0:T(8,128)S(1)}, u32[]{:S(2)}, u32[]{:S(2)}) collective-permute-start(f32[8,256]{1,0:T(8,128)S(1)} %shard_map.151.mine), channel_id=1, source_target_pairs={{0,8},{8,0},{16,24},{24,16},{32,40},{40,32},{48,56},{56,48},{64,72... | collective-permute-start | bytes 24584 | tf_op jit(solution)/shard_map/ppermute | solution.py:442
  126.1 0.0 collective-permute-done.4
  126.1 0.0 collective-permute-done.6
  126.1 1.8 %pad_maximum_fusion = f32[8,16384]{1,0:T(8,128)} fusion(f32[8,8192]{1,0:T(8,128)} %collective-permute-done.6, f32[8,8192]{1,0:T(8,128)S(1)} %collective-permute-done.4), kind=kLoop, calls=%fused_computation | loop fusion | flops 131072 | bytes 1048576 | tf_op jit(solution)/shard_map/concatenate | solution.py:422
  127.9 0.0 collective-permute-done.2.nxt
  127.9 0.6 copy-done.15
  128.5 1.4 %seam.1 = (f32[512,256]{1,0:T(8,128)}, f32[512,256]{1,0:T(8,128)}) custom-call(f32[512,256]{1,0:T(8,128)} %get-tuple-element.31.gk_in, f32[512,256]{1,0:T(8,128)} %get-tuple-element.32.gv_in, f32[2,2,256]{2,1,0:T(2,128)} %copy-done.15, f32[3,3,256]{2,1,0:T(4,128)} %taps.7), custom_call_target="tpu_custom_call", output_to_operand_aliasing={{0}: (0, {}), {1}: (1, {})} | custom-call | tf_op jit(solution)/shard_map/seam/pallas_call | solution.py:444
  129.8 0.0 collective-permute-done.8.other
  129.8 1.2 shard_map.152
  (22 shorter events, 0.1 us)
Async XLA Ops:
  0.6 7.5 %copy-start.1 = (f32[512,256]{1,0:T(8,128)S(1)}, f32[512,256]{1,0:T(8,128)}, u32[]{:S(2)}) copy-start(f32[512,256]{1,0:T(8,128)} %v.7) | copy-start | bytes 1572868
  0.6 7.5 %copy-start = (f32[512,256]{1,0:T(8,128)S(1)}, f32[512,256]{1,0:T(8,128)}, u32[]{:S(2)}) copy-start(f32[512,256]{1,0:T(8,128)} %k.7) | copy-start | bytes 1572868
  0.7 7.4 %copy-start.3 = (f32[512,256]{1,0:T(8,128)S(1)}, f32[512,256]{1,0:T(8,128)}, u32[]{:S(2)}) copy-start(f32[512,256]{1,0:T(8,128)} %go.5) | copy-start | bytes 1572868
  0.7 7.4 %copy-start.2 = (f32[512,256]{1,0:T(8,128)S(1)}, f32[512,256]{1,0:T(8,128)}, u32[]{:S(2)}) copy-start(f32[512,256]{1,0:T(8,128)} %q.5) | copy-start | bytes 1572868
  0.7 7.4 %copy-start.10 = (f32[3,3,256]{2,1,0:T(4,128)S(1)}, f32[3,3,256]{2,1,0:T(4,128)}, u32[]{:S(2)}) copy-start(f32[3,3,256]{2,1,0:T(4,128)} %taps.7) | copy-start | bytes 27652
  0.7 7.4 %copy-start.5 = (f32[512,256]{1,0:T(8,128)S(1)}, f32[512,256]{1,0:T(8,128)}, u32[]{:S(2)}) copy-start(f32[512,256]{1,0:T(8,128)} %fil.1) | copy-start | bytes 1572868
  2.2 5.9 %collective-permute-start = (f32[8,256]{1,0:T(8,128)}, f32[8,256]{1,0:T(8,128)S(1)}, u32[]{:S(2)}, u32[]{:S(2)}) collective-permute-start(f32[8,256]{1,0:T(8,128)} %get-tuple-element.24), channel_id=1, source_target_pairs={{0,8},{8,16},{16,24},{24,32},{32,40},{40,48},{48,56},{56,64},{64,7... | collective-permute-start | bytes 24584 | tf_op jit(solution)/shard_map/ppermute | solution.py:356
  10.9 11.8 %copy-start.16 = (f32[8,256]{1,0:T(8,128)S(1)}, f32[8,256]{1,0:T(8,128)}, u32[]{:S(2)}) copy-start(f32[8,256]{1,0:T(8,128)} %get-tuple-element.25) | copy-start | bytes 24580
  11.0 48.3 %copy-start.4 = (f32[512,256]{1,0:T(8,128)S(1)}, f32[512,256]{1,0:T(8,128)}, u32[]{:S(2)}) copy-start(f32[512,256]{1,0:T(8,128)} %cs.3) | copy-start | bytes 1572868
  11.0 48.3 %copy-start.11 = (f32[256]{0:T(256)S(1)}, f32[256]{0:T(256)}, u32[]{:S(2)}) copy-start(f32[256]{0:T(256)} %param.15) | copy-start | bytes 3076
  11.0 51.8 %all-to-all-start = ((f32[32,4,24,128]{3,2,1,0:T(8,128)}), f32[32,4,24,128]{3,2,1,0:T(8,128)}, u32[]{:S(2)}, u32[]{:S(2)}) async-start(f32[32,4,24,128]{3,2,1,0:T(8,128)} %shard_map.146), calls=%async_computation | async-start | bytes 3145728 | tf_op jit(solution)/shard_map/all_to_all | solution.py:388
  22.7 40.1 %copy-start.14 = (f32[256,128]{1,0:T(8,128)S(1)}, f32[256,128]{1,0:T(8,128)}, u32[]{:S(2)}) copy-start(f32[256,128]{1,0:T(8,128)} %constant.16.clone.twist) | copy-start | bytes 393220
  22.7 36.5 %collective-permute-start.1 = (f32[8,256]{1,0:T(8,128)S(1)}, f32[8,256]{1,0:T(8,128)S(1)}, u32[]{:S(2)}, u32[]{:S(2)}) collective-permute-start(f32[8,256]{1,0:T(8,128)S(1)} %copy-done.16), channel_id=1, source_target_pairs={{8,0},{16,8},{24,16},{32,24},{40,32},{48,40},{56,48},{64,56},{72,6... | collective-permute-start | bytes 24584 | tf_op jit(solution)/shard_map/ppermute | solution.py:356
  61.2 0.8 copy-start.6
  62.0 0.8 copy-start.8
  62.8 1.2 copy-start.12
  70.3 33.5 %all-to-all-start.1 = ((f32[32,4,8,128]{3,2,1,0:T(8,128)}), f32[32,4,8,128]{3,2,1,0:T(8,128)S(1)}, u32[]{:S(2)}, u32[]{:S(2)}) async-start(f32[32,4,8,128]{3,2,1,0:T(8,128)} %bitcast.4), calls=%async_computation.1 | async-start | bytes 1048576 | tf_op jit(solution)/shard_map/all_to_all | solution.py:407
  77.1 1.2 copy-start.13
  78.3 25.6 %copy-start.7 = (f32[512,256]{1,0:T(8,128)S(1)}, f32[512,256]{1,0:T(8,128)}, u32[]{:S(2)}) copy-start(f32[512,256]{1,0:T(8,128)} %copy-done.6) | copy-start | bytes 1572868
  78.3 25.6 %copy-start.9 = (f32[512,256]{1,0:T(8,128)S(1)}, f32[512,256]{1,0:T(8,128)}, u32[]{:S(2)}) copy-start(f32[512,256]{1,0:T(8,128)} %copy-done.8) | copy-start | bytes 1572868
  84.0 10.6 %collective-permute-start.3 = (f32[8,8192]{1,0:T(8,128)S(1)}, f32[8,8192]{1,0:T(8,128)}, u32[]{:S(2)}, u32[]{:S(2)}) collective-permute-start(f32[8,8192]{1,0:T(8,128)S(1)} %get-tuple-element.36), channel_id=1, source_target_pairs={{0,0},{1,2},{2,1},{3,3},{4,4},{5,6},{6,5},{7,7},{8,13},{9,15},{10,... | collective-permute-start | bytes 786440 | tf_op jit(solution)/shard_map/ppermute | solution.py:419
  91.0 8.4 %collective-permute-start.5 = (f32[8,8192]{1,0:T(8,128)S(1)}, f32[8,8192]{1,0:T(8,128)}, u32[]{:S(2)}, u32[]{:S(2)}) collective-permute-start(f32[8,8192]{1,0:T(8,128)S(1)} %get-tuple-element.37), channel_id=1, source_target_pairs={{0,0},{1,2},{2,1},{3,3},{4,4},{5,6},{6,5},{7,7},{8,13},{9,15},{10,... | collective-permute-start | bytes 786440 | tf_op jit(solution)/shard_map/ppermute | solution.py:419
  94.7 31.4 %collective-permute-start.4 = (f32[8,8192]{1,0:T(8,128)}, f32[8,8192]{1,0:T(8,128)S(1)}, u32[]{:S(2)}, u32[]{:S(2)}) collective-permute-start(f32[8,8192]{1,0:T(8,128)} %collective-permute-done.3), channel_id=1, source_target_pairs={{0,0},{2,34},{1,81},{3,115},{4,132},{6,166},{5,213},{7,247},{13,13... | collective-permute-start | bytes 786440 | tf_op jit(solution)/shard_map/ppermute | solution.py:420
  99.4 26.7 %collective-permute-start.6 = (f32[8,8192]{1,0:T(8,128)}, f32[8,8192]{1,0:T(8,128)}, u32[]{:S(2)}, u32[]{:S(2)}) collective-permute-start(f32[8,8192]{1,0:T(8,128)} %collective-permute-done.5), channel_id=1, source_target_pairs={{0,0},{2,34},{1,81},{3,115},{4,132},{6,166},{5,213},{7,247},{13,13... | collective-permute-start | bytes 786440 | tf_op jit(solution)/shard_map/ppermute | solution.py:421
  106.3 1.2 collective-permute-start.7
  108.2 16.2 %all-to-all-start.2 = ((f32[16,1,1280]{2,1,0:T(1,128)}), f32[16,1,1280]{2,1,0:T(1,128)S(1)}, u32[]{:S(2)}, u32[]{:S(2)}) async-start(f32[16,1,1280]{2,1,0:T(1,128)} %shard_map.150), calls=%async_computation.2 | async-start | bytes 163840 | tf_op jit(solution)/shard_map/all_to_all | solution.py:438
  117.0 10.9 %collective-permute-start.2 = (f32[2,2,256]{2,1,0:T(2,128)S(1)}, f32[2,2,256]{2,1,0:T(2,128)S(1)}, u32[]{:S(2)}, u32[]{:S(2)}) collective-permute-start(f32[2,2,256]{2,1,0:T(2,128)S(1)} %get-tuple-element.33), channel_id=1, source_target_pairs={{8,0},{16,8},{24,16},{32,24},{40,32},{48,40},{56,48},{64,56},{72,6... | collective-permute-start | bytes 12296 | tf_op jit(solution)/shard_map/ppermute | solution.py:356
  124.4 5.4 %collective-permute-start.8 = (f32[8,256]{1,0:T(8,128)S(1)}, f32[8,256]{1,0:T(8,128)S(1)}, u32[]{:S(2)}, u32[]{:S(2)}) collective-permute-start(f32[8,256]{1,0:T(8,128)S(1)} %shard_map.151.mine), channel_id=1, source_target_pairs={{0,8},{8,0},{16,24},{24,16},{32,40},{40,32},{48,56},{56,48},{64,72... | collective-permute-start | bytes 24584 | tf_op jit(solution)/shard_map/ppermute | solution.py:442
  127.9 0.6 copy-start.15

commit v2 on v1

--- a/solution.py
+++ b/solution.py
@@ -147,12 +147,10 @@
     correlate(blocks, 0, src, tab, twist, out, *scratch)
 
 
-def second_kernel(blocks, src, tab, twist, early, late, held, *scratch):
+def second_kernel(blocks, src, tab, twist, out, held, *scratch):
     correlate(blocks, 2, src, tab, twist, held, *scratch)
-    half = 2 * blocks
-    for a in range(half):
-        early[:, a * LANES : (a + 1) * LANES] = held[a * 8 : (a + 1) * 8, :]
-        late[:, a * LANES : (a + 1) * LANES] = held[(half + a) * 8 : (half + a + 1) * 8, :]
+    for a in range(4 * blocks):
+        out[:, a * LANES : (a + 1) * LANES] = held[a * 8 : (a + 1) * 8, :]
 
 
 def put_ext(ext, i, prev, x):
@@ -168,14 +166,13 @@
     )
 
 
-def edge_kernel(q, k, v, go, cs, tails, heads):
+def edge_kernel(q, k, v, tails):
     for i, x in enumerate((q, k, v)):
         tails[2 * i : 2 * i + 2, :] = x[6:8, :]
     tails[6:8, :] = jnp.zeros((2, q.shape[1]), f32)
-    heads[...] = go[...] * cs[...]
-
-
-def send_kernel(t_ref, taps, prev, q, k, v, go, fil, out, ext, gof, sems):
+
+
+def send_kernel(t_ref, taps, prev_in, q, k, v, go, fil, out, ext, gof, prev, sems):
     n = q.shape[0]
     copies = [
         pltpu.make_async_copy(src, dst, sems.at[i])
@@ -186,14 +183,13 @@
                 (v, ext.at[2, pl.ds(8, n)]),
                 (q, ext.at[0, pl.ds(8, n)]),
                 (go, gof.at[1]),
+                (prev_in, prev),
             )
         )
     ]
     for c in copies:
         c.start()
     t = t_ref[0]
-    for i in range(3):
-        ext[i, 6:8, :] = prev[2 * i : 2 * i + 2, :]
     groups = out.shape[0]
     owners = [owner_of(g, t) for g in range(groups)]
 
@@ -206,6 +202,9 @@
     copies[0].wait()
     for r0 in starts:
         put(0, r0, gof[0, r0 : r0 + LANES, :])
+    copies[5].wait()
+    for i in range(3):
+        ext[i, 6:8, :] = prev[2 * i : 2 * i + 2, :]
     copies[1].wait()
     copies[2].wait()
     for r0 in starts:
@@ -217,12 +216,12 @@
 
 
 def side_kernel(
-    taps, prev, q, k, v, go, cs, gain, following, zbase, ks, vs, gq, sums, ext, gext
+    taps, prev, q, k, v, go, cs, gain, zbase, ks, vs, gq, sums, ext, gext
 ):
     n = q.shape[0]
     for i, x in enumerate((q, k, v)):
         put_ext(ext, i, prev, x)
-    gext[n : n + 8, :] = following[...]
+    gext[n:, :] = jnp.zeros((8, q.shape[1]), f32)
     for r0 in range(0, n, LANES):
         gext[r0 : r0 + LANES, :] = go[r0 : r0 + LANES, :] * cs[r0 : r0 + LANES, :]
     totals = [jnp.zeros((1, q.shape[1]), f32) for _ in range(4)]
@@ -247,25 +246,42 @@
         totals[3] += jnp.sum(gw * (k_short * v_short), axis=0, keepdims=True)
     for o in range(4):
         sums[o : o + 1, :] = totals[o]
-    sums[4:, :] = jnp.zeros((4, q.shape[1]), f32)
+    sums[4:6, :] = gext[0:2, :]
+    sums[6:8, :] = jnp.zeros((2, q.shape[1]), f32)
 
 
 def last_kernel(
-    t_ref, corr, zbase, ks, vs, taps, prev, k, v, early, gk, gv, heads, keep, give, ext, gext, held
+    t_ref, corr, zbase_in, ks_in, vs_in, taps, prev, k, v, early,
+    gk, gv, heads, keep, give, ext, gext, held, base, sems,
 ):
     t = t_ref[0]
     n = k.shape[0]
+    steps = []
+    for j, r0 in enumerate(range(0, n, LANES)):
+        rows = pl.ds(r0, LANES)
+        pairs = [(x.at[rows], base.at[i, rows]) for i, x in enumerate((zbase_in, ks_in, vs_in))]
+        pairs += [
+            (x.at[rows], ext.at[i, pl.ds(8 + r0, LANES)]) for i, x in enumerate((k, v))
+        ]
+        steps.append(
+            [pltpu.make_async_copy(x, y, sems.at[5 * j + i]) for i, (x, y) in enumerate(pairs)]
+        )
+    for step in steps:
+        for c in step:
+            c.start()
+    zbase, ks, vs = base.at[0], base.at[1], base.at[2]
     groups = corr.shape[0]
     owners = [owner_of(g, t) for g in range(groups)]
-    for i, x in enumerate((k, v)):
+    for i in range(2):
         ext[i, 6:8, :] = prev[2 * i + 2 : 2 * i + 4, :]
-        ext[i, 8:, :] = x[...]
         gext[i, n:, :] = jnp.zeros((8, k.shape[1]), f32)
     totals = [jnp.zeros((1, k.shape[1]), f32) for _ in range(6)]
     for r0 in range(0, n, LANES):
         rows = slice(r0, r0 + LANES)
         for g in range(groups):
             held[g * 8 : g * 8 + 8, :] = corr[owners[g], r0 // LANES]
+        for c in steps[r0 // LANES]:
+            c.wait()
         grad_z = zbase[rows, :] + jnp.transpose(held[...])
         for i, other in enumerate((vs, ks)):
             g = grad_z * other[rows, :]
@@ -282,8 +298,10 @@
         give[o : o + 1, :] = jnp.where(even, totals[5 + o], totals[o])
     for x in (keep, give):
         x[5:8, :] = jnp.zeros((3, width), f32)
+    heads[0:2, :] = early[4:6, :]
+    heads[6:8, :] = jnp.zeros((2, width), f32)
     for i, out in enumerate((gk, gv)):
-        heads[i] = gext[i, 0:2, :]
+        heads[2 * i + 2 : 2 * i + 4, :] = gext[i, 0:2, :]
         for r0 in range(0, n, LANES):
             out[r0 : r0 + LANES, :] = (
                 taps[i + 1, 0:1, :] * gext[i, r0 : r0 + LANES, :]
@@ -292,10 +310,10 @@
             )
 
 
-def seam_kernel(gk_in, gv_in, nxt, taps, gk, gv):
-    for i, (src, dst) in enumerate(((gk_in, gk), (gv_in, gv))):
-        one, two = taps[i + 1, 1:2, :], taps[i + 1, 2:3, :]
-        first, second = nxt[i, 0:1, :], nxt[i, 1:2, :]
+def seam_kernel(gq_in, gk_in, gv_in, nxt, taps, gq, gk, gv):
+    for i, (src, dst) in enumerate(((gq_in, gq), (gk_in, gk), (gv_in, gv))):
+        one, two = taps[i, 1:2, :], taps[i, 2:3, :]
+        first, second = nxt[2 * i : 2 * i + 1, :], nxt[2 * i + 1 : 2 * i + 2, :]
         dst[...] = src[...]
         dst[6:7, :] = src[6:7, :] + two * first
         dst[7:8, :] = src[7:8, :] + one * first + two * second
@@ -338,7 +356,7 @@
     return jax.ShapeDtypeStruct(s, f32)
 
 
-def call(body, ins, outs, args, scratch=(), flops=10**6, nbytes=4 * 10**6):
+def call(body, ins, outs, args, scratch=(), flops=10**6, nbytes=4 * 10**6, room=40):
     return pl.pallas_call(
         body,
         out_shape=outs,
@@ -346,7 +364,7 @@
         out_specs=jax.tree.map(lambda _: VM, outs),
         scratch_shapes=list(scratch),
         cost_estimate=pl.CostEstimate(flops=flops, bytes_accessed=nbytes, transcendentals=0),
-        compiler_params=pltpu.CompilerParams(vmem_limit_bytes=40 * 2**20),
+        compiler_params=pltpu.CompilerParams(vmem_limit_bytes=room * 2**20),
     )(*args)
 
 
@@ -368,22 +386,24 @@
 
     low = pl.BlockSpec((8, width), lambda i: (n // 8 - 1, 0))
     top = pl.BlockSpec((8, width), lambda i: (0, 0))
-    tails, heads = pl.pallas_call(
+    tails = pl.pallas_call(
         edge_kernel,
         grid=(1,),
-        out_shape=(shape(8, width), shape(8, width)),
-        in_specs=[low, low, low, top, top],
-        out_specs=(top, top),
+        out_shape=shape(8, width),
+        in_specs=[low, low, low],
+        out_specs=top,
         name="edge",
-    )(q, k, v, go, cs)
+    )(q, k, v)
     prev = shifted(tails, 1)
-    nxt_q = shifted(heads, -1)
 
     ext3 = pltpu.VMEM((3, n + 8, width), f32)
     packed = call(
-        send_kernel, [SM, VM, VM] + [HB] * 5, shape(blocks, n // LANES, 24, LANES),
+        send_kernel, [SM, VM] + [HB] * 6, shape(blocks, n // LANES, 24, LANES),
         (t, taps, prev, q, k, v, go, fil),
-        [ext3, pltpu.VMEM((2, n, width), f32), pltpu.SemaphoreType.DMA((5,))],
+        [
+            ext3, pltpu.VMEM((2, n, width), f32), pltpu.VMEM((8, width), f32),
+            pltpu.SemaphoreType.DMA((6,)),
+        ], room=62,
     )
     arrived = lax.all_to_all(packed, "ctx", 0, 0, tiled=True)
     arrived = arrived.reshape(seq // LANES, 24, LANES)
@@ -394,21 +414,21 @@
         pltpu.SemaphoreType.DMA((4,)),
     ]
     zbase, ks, vs, gq, early = call(
-        side_kernel, [VM] * 9,
+        side_kernel, [VM] * 8,
         (shape(n, width),) * 4 + (shape(8, width),),
-        (taps, prev, q, k, v, go, cs, gain.reshape(1, width), nxt_q),
+        (taps, prev, q, k, v, go, cs, gain.reshape(1, width)),
         [ext3, pltpu.VMEM((n + 8, width), f32)],
     )
     corr = call(
         functools.partial(first_kernel, blocks), [HB, TB, TB, HB],
         shape(seq * 8 // LANES, LANES), (arrived, *tabs, early), work,
-        flops=2 * 10**9,
+        flops=2 * 10**9, room=62,
     )
     back = lax.all_to_all(corr.reshape(blocks, n // LANES, 8, LANES), "ctx", 0, 0, tiled=True)
     zeta = call(
         functools.partial(second_kernel, blocks), [HB, TB, TB],
-        (shape(8, seq // 2), shape(8, seq // 2)), (arrived, *tabs),
-        [pltpu.VMEM((seq * 8 // LANES, LANES), f32), *work], flops=2 * 10**9,
+        shape(8, seq), (arrived, *tabs),
+        [pltpu.VMEM((seq * 8 // LANES, LANES), f32), *work], flops=2 * 10**9, room=62,
     )
     hop_one, hop_two = [], []
     for c in range(blocks):
@@ -416,20 +436,20 @@
             row, column = target_of(c, s)
             hop_one.append((c * tp + s, c * tp + column))
             hop_two.append((c * tp + column, row * tp + column))
-    zeta = [lax.ppermute(x, ("ctx", "tp"), hop_one) for x in zeta]
-    early_half = lax.ppermute(zeta[0], ("ctx", "tp"), hop_two)
-    late_half = lax.ppermute(zeta[1], ("ctx", "tp"), hop_two)
-    grad_filter = jnp.concatenate([early_half, late_half], axis=1)
+    zeta = lax.ppermute(zeta, ("ctx", "tp"), hop_one)
+    grad_filter = lax.ppermute(zeta, ("ctx", "tp"), hop_two)
 
     gk, gv, heads, keep, give = call(
-        last_kernel, [SM] + [VM] * 9,
-        (shape(n, width), shape(n, width), shape(2, 2, width), shape(8, width), shape(8, width)),
+        last_kernel, [SM, VM, HB, HB, HB, VM, VM, HB, HB, VM],
+        (shape(n, width), shape(n, width), shape(8, width), shape(8, width), shape(8, width)),
         (t, back, zbase, ks, vs, taps, prev, k, v, early),
         [
             pltpu.VMEM((2, n + 8, width), f32),
             pltpu.VMEM((2, n + 8, width), f32),
             pltpu.VMEM((width, LANES), f32),
-        ],
+            pltpu.VMEM((3, n, width), f32),
+            pltpu.SemaphoreType.DMA((5 * (n // LANES),)),
+        ], room=60,
     )
     swap = [(i, i ^ 1) for i in range(blocks)]
     got = lax.ppermute(give, "ctx", swap)
@@ -441,15 +461,15 @@
     total = call(gather_kernel, [VM], shape(8, width), (parts,))
     other = lax.ppermute(total, "ctx", swap)
     nxt = shifted(heads, -1)
-    gk, gv = pl.pallas_call(
+    gq, gk, gv = pl.pallas_call(
         seam_kernel,
         grid=(1,),
-        out_shape=(shape(n, width), shape(n, width)),
-        in_specs=[low, low, VM, VM],
-        out_specs=(low, low),
-        input_output_aliases={0: 0, 1: 1},
+        out_shape=(shape(n, width),) * 3,
+        in_specs=[low, low, low, VM, VM],
+        out_specs=(low, low, low),
+        input_output_aliases={0: 0, 1: 1, 2: 2},
         name="seam",
-    )(gk, gv, nxt, taps)
+    )(gq, gk, gv, nxt, taps)
     grad_taps, grad_skip = call(
         finish_kernel, [SM, VM, VM], (shape(3, 3, width), shape(1, width)), (t, total, other),
     )

time: 133 us -> 131 us (0.985)
  starting transfers between devices: 54 us -> 45.4 us
  Pallas kernels: 24 us -> 28.3 us
  local copies, waits for them, and re-layouts: 4.55 us -> 6.53 us
    ppermute x3 -> x2, waiting for transfers between devices: 35.1 us -> 0.31 us  [shifted(): return lax.ppermute(value, 'ctx', pairs)]
    all_to_all x1, waiting for transfers between devices: 0.01 us -> 33.3 us  [on_device(): arrived = lax.all_to_all(packed, 'ctx', 0, 0, tiled=True)]
    ppermute x4 -> x2, starting transfers between devices: 15.4 us -> 8.9 us  [the longest x1 6.99 us: on_device(): zeta = lax.ppermute(zeta, ('ctx', 'tp'), hop_one)]
    pallas_call x8, Pallas kernels: 21.1 us -> 25.6 us  [call(): pl.pallas_call(body, out_shape=outs, in_specs=ins, out_specs=jax.tree.map...]
    ppermute x4 -> x2, waiting for transfers between devices: 4.43 us -> 6.77 us  [the longest x1 6.77 us: on_device(): zeta = lax.ppermute(zeta, ('ctx', 'tp'), hop_one)]
    ppermute x3 -> x2, starting transfers between devices: 9.61 us -> 7.27 us  [shifted(): return lax.ppermute(value, 'ctx', pairs)]
    unnamed x34 -> x35, local copies, waits for them, and re-layouts: 4.55 us -> 6.53 us
    concatenate x1 -> x0, other arithmetic: 1.78 us -> none  [on_device(): grad_filter = jnp.concatenate([early_half, late_half], axis=1)]
  transfers between devices with their start and end apart: 12 -> 9, of which waited for: 6 -> 5; matrix products, arithmetic and copies ran while one was open for 1% -> 1% of each run, Pallas kernels for 9% -> 12%
where the time goes in v2:
time: 131 us; the launch traced here: 129 us
  waiting for transfers between devices  46.9 us (36%)
  starting transfers between devices  45.4 us (35%)
  Pallas kernels  28.3 us (22%)
  local copies, waits for them, and re-layouts  6.53 us (5%)
    all_to_all x1, waiting for transfers between devices, on_device(): arrived = lax.all_to_all(packed, 'ctx', 0, 0, tiled=True)  33.3 us
    pallas_call x8, Pallas kernels, call(): pl.pallas_call(body, out_shape=outs, in_specs=ins, out_specs=jax.tree.map...  25.6 us
    all_to_all x1, starting transfers between devices, on_device(): arrived = lax.all_to_all(packed, 'ctx', 0, 0, tiled=True)  11.7 us
    all_to_all x1, starting transfers between devices, on_device(): lax.all_to_all(parts, 'ctx', 0, 0, axis_index_groups=same, tiled=True)  10.4 us
    ppermute x2, starting transfers between devices, shifted(): return lax.ppermute(value, 'ctx', pairs)  7.27 us
    ppermute x1, starting transfers between devices, on_device(): zeta = lax.ppermute(zeta, ('ctx', 'tp'), hop_one)  6.99 us
    ppermute x1, waiting for transfers between devices, on_device(): zeta = lax.ppermute(zeta, ('ctx', 'tp'), hop_one)  6.77 us
    unnamed x35, local copies, waits for them, and re-layouts  6.53 us
  transfers between devices with their start and end apart: 9, of which 5 were waited for; matrix products, arithmetic and copies ran while one was open for 1% of the time, Pallas kernels for 12%

profile of v2, /device:TPU:1, one launch (start us, length us, event | category | flops | bytes accessed | tf_op | source)
XLA Modules:
  0.0 128.7 jit_solution(3933761283050717171)
XLA Ops:
  0.6 1.3 %edge.1 = f32[8,256]{1,0:T(8,128)} custom-call(f32[512,256]{1,0:T(8,128)} %q.5, f32[512,256]{1,0:T(8,128)} %k.7, f32[512,256]{1,0:T(8,128)} %v.7), custom_call_target="tpu_custom_call" | custom-call | tf_op jit(solution)/shard_map/edge/pallas_call | solution.py:389
  2.0 4.9 %collective-permute-start = (f32[8,256]{1,0:T(8,128)}, f32[8,256]{1,0:T(8,128)S(1)}, u32[]{:S(2)}, u32[]{:S(2)}) collective-permute-start(f32[8,256]{1,0:T(8,128)} %edge.1), channel_id=1, source_target_pairs={{0,8},{8,16},{16,24},{24,32},{32,40},{40,48},{48,56},{56,64},{64,7... | collective-permute-start | bytes 24584 | tf_op jit(solution)/shard_map/ppermute | solution.py:374
  6.9 0.7 pad_add_fusion.t_ref
  7.6 0.3 collective-permute-done.prev.prev_in
  7.9 0.6 copy-done.9
  8.5 4.1 %shard_map.146 = f32[32,4,24,128]{3,2,1,0:T(8,128)} custom-call(s32[2]{0:T(128)} %pad_add_fusion.t_ref, f32[3,3,256]{2,1,0:T(4,128)} %taps.7, f32[8,256]{1,0:T(8,128)} %copy-done.9, f32[512,256]{1,0:T(8,128)} %q.5, f32[512,256]{1,0:T(8,128)} %k.7, f32[512,256]{1,0:T(8,128)} %v.7, f32[512,256]{1,0:T(8,128)} %go.3, f32[512,256]{1,0:T(8,128)} %fil.1), custom_call_target="tpu_custom_call" | custom-call | flops 1000000 | bytes 4000000 | tf_op jit(solution)/shard_map/pallas_call | solution.py:360
  12.5 0.0 copy-start
  12.5 0.0 copy-start.1
  12.6 0.0 copy-start.2
  12.6 0.0 copy-start.3
  12.6 0.0 copy-start.4
  12.6 0.0 copy-start.8
  12.6 0.0 copy-start.10
  12.6 0.0 copy-start.14
  12.6 11.7 %all-to-all-start = ((f32[32,4,24,128]{3,2,1,0:T(8,128)}), f32[32,4,24,128]{3,2,1,0:T(8,128)}, u32[]{:S(2)}, u32[]{:S(2)}) async-start(f32[32,4,24,128]{3,2,1,0:T(8,128)} %shard_map.146), calls=%async_computation | async-start | bytes 3145728 | tf_op jit(solution)/shard_map/all_to_all | solution.py:408
  24.4 0.0 copy-done
  24.4 0.0 copy-done.1
  24.4 1.9 %shard_map.145 = (f32[512,256]{1,0:T(8,128)S(1)}, f32[512,256]{1,0:T(8,128)S(1)}, f32[512,256]{1,0:T(8,128)S(1)}, f32[512,256]{1,0:T(8,128)}, f32[8,256]{1,0:T(8,128)S(1)}) custom-call(f32[3,3,256]{2,1,0:T(4,128)S(1)} %copy-done.8, f32[8,256]{1,0:T(8,128)S(1)} %copy-done.10, f32[512,256]{1,0:T(8,128)S(1)} %copy-done.2, f32[512,256]{1,0:T(8,128)S(1)} %copy-done, ...), custom_call_target="tpu_custom_call" | custom-call | flops 1000000 | bytes 4000000 | tf_op jit(solution)/shard_map/pallas_call | solution.py:360
  26.4 0.8 copy-done.5
  27.2 0.8 copy-done.6
  28.0 0.8 copy-done.7
  28.8 0.6 copy-done.11
  29.4 33.3 %all-to-all-done = f32[32,4,24,128]{3,2,1,0:T(8,128)} async-done(((f32[32,4,24,128]{3,2,1,0:T(8,128)}), f32[32,4,24,128]{3,2,1,0:T(8,128)}, u32[]{:S(2)}, u32[]{:S(2)}) %all-to-all-start) | async-done | bytes 1572896 | tf_op jit(solution)/shard_map/all_to_all | solution.py:408
  62.6 6.7 %shard_map.147 = f32[1024,128]{1,0:T(8,128)} custom-call(f32[128,24,128]{2,1,0:T(8,128)} %bitcast.3.src, bf16[1664,256]{1,0:T(8,128)(2,1)} %constant.15.clone.tab, f32[256,128]{1,0:T(8,128)} %constant.16.clone.twist, f32[8,256]{1,0:T(8,128)} %copy-done.11), custom_call_target="tpu_custom_call" | custom-call | flops 2000000000 | bytes 4000000 | tf_op jit(solution)/shard_map/pallas_call | solution.py:360
  69.3 5.5 %all-to-all-start.1 = ((f32[32,4,8,128]{3,2,1,0:T(8,128)}), f32[32,4,8,128]{3,2,1,0:T(8,128)S(1)}, u32[]{:S(2)}, u32[]{:S(2)}) async-start(f32[32,4,8,128]{3,2,1,0:T(8,128)} %bitcast.7), calls=%async_computation.1 | async-start | bytes 1048576 | tf_op jit(solution)/shard_map/all_to_all | solution.py:427
  74.7 6.7 %shard_map.149 = f32[8,16384]{1,0:T(8,128)} custom-call(f32[128,24,128]{2,1,0:T(8,128)} %bitcast.3.src, bf16[1664,256]{1,0:T(8,128)(2,1)} %constant.15.clone.tab, f32[256,128]{1,0:T(8,128)} %constant.16.clone.twist), custom_call_target="tpu_custom_call" | custom-call | flops 2000000000 | bytes 4000000 | tf_op jit(solution)/shard_map/pallas_call | solution.py:360
  81.5 7.0 %collective-permute-start.2 = (f32[8,16384]{1,0:T(8,128)}, f32[8,16384]{1,0:T(8,128)S(1)}, u32[]{:S(2)}, u32[]{:S(2)}) collective-permute-start(f32[8,16384]{1,0:T(8,128)} %shard_map.149), channel_id=1, source_target_pairs={{0,0},{1,2},{2,1},{3,3},{4,4},{5,6},{6,5},{7,7},{8,13},{9,15},{10,... | collective-permute-start | bytes 1572872 | tf_op jit(solution)/shard_map/ppermute | solution.py:439
  88.5 6.8 %collective-permute-done.2 = f32[8,16384]{1,0:T(8,128)S(1)} collective-permute-done((f32[8,16384]{1,0:T(8,128)}, f32[8,16384]{1,0:T(8,128)S(1)}, u32[]{:S(2)}, u32[]{:S(2)}) %collective-permute-start.2) | collective-permute-done | bytes 524320 | tf_op jit(solution)/shard_map/ppermute | solution.py:439
  95.2 1.9 %collective-permute-start.3 = (f32[8,16384]{1,0:T(8,128)S(1)}, f32[8,16384]{1,0:T(8,128)S(1)}, u32[]{:S(2)}, u32[]{:S(2)}) collective-permute-start(f32[8,16384]{1,0:T(8,128)S(1)} %collective-permute-done.2), channel_id=1, source_target_pairs={{0,0},{2,34},{1,81},{3,115},{4,132},{6,166},{5,213},{7,247},{13,13... | collective-permute-start | bytes 1572872 | tf_op jit(solution)/shard_map/ppermute | solution.py:440
  97.2 0.0 all-to-all-done.1.corr
  97.2 0.0 copy-start.15
  97.2 0.8 copy-done.15
  98.0 4.4 %shard_map.148 = (f32[512,256]{1,0:T(8,128)}, f32[512,256]{1,0:T(8,128)}, f32[8,256]{1,0:T(8,128)}, f32[8,256]{1,0:T(8,128)}, f32[8,256]{1,0:T(8,128)}) custom-call(s32[2]{0:T(128)} %pad_add_fusion.t_ref, f32[32,4,8,128]{3,2,1,0:T(8,128)} %copy-done.15, f32[512,256]{1,0:T(8,128)} %copy-done.5, f32[512,256]{1,0:T(8,128)} %copy-done.6, f32[512,256]{1,0:T(8,128)} %copy-done.7, ...), custom_call_target="tpu_custom_call" | custom-call | flops 1000000 | bytes 4000000 | tf_op jit(solution)/shard_map/pallas_call | solution.py:360
  102.4 0.1 collective-permute-start.4
  102.5 1.4 %collective-permute-done.4.got = f32[8,256]{1,0:T(8,128)S(1)} collective-permute-done((f32[8,256]{1,0:T(8,128)}, f32[8,256]{1,0:T(8,128)S(1)}, u32[]{:S(2)}, u32[]{:S(2)}) %collective-permute-start.4) | collective-permute-done | bytes 8224 | tf_op jit(solution)/shard_map/ppermute | solution.py:455
  103.8 0.7 copy-done.12
  104.5 0.7 shard_map.150
  105.2 10.4 %all-to-all-start.2 = ((f32[16,1,1280]{2,1,0:T(1,128)}), f32[16,1,1280]{2,1,0:T(1,128)S(1)}, u32[]{:S(2)}, u32[]{:S(2)}) async-start(f32[16,1,1280]{2,1,0:T(1,128)} %shard_map.150), calls=%async_computation.2 | async-start | bytes 163840 | tf_op jit(solution)/shard_map/all_to_all | solution.py:458
  115.6 2.4 %collective-permute-start.1 = (f32[8,256]{1,0:T(8,128)}, f32[8,256]{1,0:T(8,128)S(1)}, u32[]{:S(2)}, u32[]{:S(2)}) collective-permute-start(f32[8,256]{1,0:T(8,128)} %get-tuple-element.28), channel_id=1, source_target_pairs={{8,0},{16,8},{24,16},{32,24},{40,32},{48,40},{56,48},{64,56},{72,6... | collective-permute-start | bytes 24584 | tf_op jit(solution)/shard_map/ppermute | solution.py:374
  118.0 5.2 %all-to-all-done.2.parts = f32[16,1,1280]{2,1,0:T(1,128)S(1)} async-done(((f32[16,1,1280]{2,1,0:T(1,128)}), f32[16,1,1280]{2,1,0:T(1,128)S(1)}, u32[]{:S(2)}, u32[]{:S(2)}) %all-to-all-start.2) | async-done | bytes 81952 | tf_op jit(solution)/shard_map/all_to_all | solution.py:458
  123.2 1.6 %collective-permute-start.5 = (f32[8,256]{1,0:T(8,128)S(1)}, f32[8,256]{1,0:T(8,128)S(1)}, u32[]{:S(2)}, u32[]{:S(2)}) collective-permute-start(f32[8,256]{1,0:T(8,128)S(1)} %shard_map.151.mine), channel_id=1, source_target_pairs={{0,8},{8,0},{16,24},{24,16},{32,40},{40,32},{48,56},{56,48},{64,72... | collective-permute-start | bytes 24584 | tf_op jit(solution)/shard_map/ppermute | solution.py:462
  124.7 0.0 collective-permute-done.1.nxt
  124.7 0.6 copy-done.16
  125.3 1.4 %seam.1 = (f32[512,256]{1,0:T(8,128)}, f32[512,256]{1,0:T(8,128)}, f32[512,256]{1,0:T(8,128)}) custom-call(f32[512,256]{1,0:T(8,128)} %get-tuple-element.21.gq_in, f32[512,256]{1,0:T(8,128)} %get-tuple-element.26.gk_in, f32[512,256]{1,0:T(8,128)} %get-tuple-element.27.gv_in, ...), custom_call_target="tpu_custom_call", output_to_operand_aliasing={{0}: (0, {}), {1}: (1, {}), {2}: (2, {})} | custom-call | tf_op jit(solution)/shard_map/seam/pallas_call | solution.py:464
  126.7 0.0 collective-permute-done.3
  126.7 0.0 collective-permute-done.5.other
  126.7 1.2 shard_map.152
  127.9 0.8 copy.23
  (16 shorter events, 0.0 us)
Async XLA Ops:
  2.0 5.9 %collective-permute-start = (f32[8,256]{1,0:T(8,128)}, f32[8,256]{1,0:T(8,128)S(1)}, u32[]{:S(2)}, u32[]{:S(2)}) collective-permute-start(f32[8,256]{1,0:T(8,128)} %edge.1), channel_id=1, source_target_pairs={{0,8},{8,16},{16,24},{24,32},{32,40},{40,48},{48,56},{56,64},{64,7... | collective-permute-start | bytes 24584 | tf_op jit(solution)/shard_map/ppermute | solution.py:374
  7.9 0.6 copy-start.9
  12.5 11.8 %copy-start = (f32[512,256]{1,0:T(8,128)S(1)}, f32[512,256]{1,0:T(8,128)}, u32[]{:S(2)}) copy-start(f32[512,256]{1,0:T(8,128)} %k.7) | copy-start | bytes 1572868
  12.5 11.8 %copy-start.1 = (f32[512,256]{1,0:T(8,128)S(1)}, f32[512,256]{1,0:T(8,128)}, u32[]{:S(2)}) copy-start(f32[512,256]{1,0:T(8,128)} %v.7) | copy-start | bytes 1572868
  12.6 11.8 %copy-start.2 = (f32[512,256]{1,0:T(8,128)S(1)}, f32[512,256]{1,0:T(8,128)}, u32[]{:S(2)}) copy-start(f32[512,256]{1,0:T(8,128)} %q.5) | copy-start | bytes 1572868
  12.6 11.8 %copy-start.3 = (f32[512,256]{1,0:T(8,128)S(1)}, f32[512,256]{1,0:T(8,128)}, u32[]{:S(2)}) copy-start(f32[512,256]{1,0:T(8,128)} %go.3) | copy-start | bytes 1572868
  12.6 11.8 %copy-start.4 = (f32[512,256]{1,0:T(8,128)S(1)}, f32[512,256]{1,0:T(8,128)}, u32[]{:S(2)}) copy-start(f32[512,256]{1,0:T(8,128)} %cs.1) | copy-start | bytes 1572868
  12.6 11.8 %copy-start.8 = (f32[3,3,256]{2,1,0:T(4,128)S(1)}, f32[3,3,256]{2,1,0:T(4,128)}, u32[]{:S(2)}) copy-start(f32[3,3,256]{2,1,0:T(4,128)} %taps.7) | copy-start | bytes 27652
  12.6 11.8 %copy-start.10 = (f32[8,256]{1,0:T(8,128)S(1)}, f32[8,256]{1,0:T(8,128)}, u32[]{:S(2)}) copy-start(f32[8,256]{1,0:T(8,128)} %copy-done.9) | copy-start | bytes 24580
  12.6 11.8 %copy-start.14 = (f32[256]{0:T(256)S(1)}, f32[256]{0:T(256)}, u32[]{:S(2)}) copy-start(f32[256]{0:T(256)} %param.15) | copy-start | bytes 3076
  12.6 50.0 %all-to-all-start = ((f32[32,4,24,128]{3,2,1,0:T(8,128)}), f32[32,4,24,128]{3,2,1,0:T(8,128)}, u32[]{:S(2)}, u32[]{:S(2)}) async-start(f32[32,4,24,128]{3,2,1,0:T(8,128)} %shard_map.146), calls=%async_computation | async-start | bytes 3145728 | tf_op jit(solution)/shard_map/all_to_all | solution.py:408
  26.4 0.8 copy-start.5
  27.2 0.8 copy-start.6
  28.0 0.8 copy-start.7
  28.8 0.6 copy-start.11
  69.3 27.9 %all-to-all-start.1 = ((f32[32,4,8,128]{3,2,1,0:T(8,128)}), f32[32,4,8,128]{3,2,1,0:T(8,128)S(1)}, u32[]{:S(2)}, u32[]{:S(2)}) async-start(f32[32,4,8,128]{3,2,1,0:T(8,128)} %bitcast.7), calls=%async_computation.1 | async-start | bytes 1048576 | tf_op jit(solution)/shard_map/all_to_all | solution.py:427
  81.5 13.8 %collective-permute-start.2 = (f32[8,16384]{1,0:T(8,128)}, f32[8,16384]{1,0:T(8,128)S(1)}, u32[]{:S(2)}, u32[]{:S(2)}) collective-permute-start(f32[8,16384]{1,0:T(8,128)} %shard_map.149), channel_id=1, source_target_pairs={{0,0},{1,2},{2,1},{3,3},{4,4},{5,6},{6,5},{7,7},{8,13},{9,15},{10,... | collective-permute-start | bytes 1572872 | tf_op jit(solution)/shard_map/ppermute | solution.py:439
  95.2 31.5 %collective-permute-start.3 = (f32[8,16384]{1,0:T(8,128)S(1)}, f32[8,16384]{1,0:T(8,128)S(1)}, u32[]{:S(2)}, u32[]{:S(2)}) collective-permute-start(f32[8,16384]{1,0:T(8,128)S(1)} %collective-permute-done.2), channel_id=1, source_target_pairs={{0,0},{2,34},{1,81},{3,115},{4,132},{6,166},{5,213},{7,247},{13,13... | collective-permute-start | bytes 1572872 | tf_op jit(solution)/shard_map/ppermute | solution.py:440
  97.2 0.8 copy-start.15
  102.3 24.4 %copy-start.13 = (s32[2]{0:T(128)S(1)}, s32[2]{0:T(128)}, u32[]{:S(2)}) copy-start(s32[2]{0:T(128)} %pad_add_fusion.t_ref) | copy-start | bytes 28
  102.4 1.5 %collective-permute-start.4 = (f32[8,256]{1,0:T(8,128)}, f32[8,256]{1,0:T(8,128)S(1)}, u32[]{:S(2)}, u32[]{:S(2)}) collective-permute-start(f32[8,256]{1,0:T(8,128)} %get-tuple-element.33), channel_id=1, source_target_pairs={{0,8},{8,0},{16,24},{24,16},{32,40},{40,32},{48,56},{56,48},{64,72... | collective-permute-start | bytes 24584 | tf_op jit(solution)/shard_map/ppermute | solution.py:455
  103.8 0.7 copy-start.12
  105.2 18.0 %all-to-all-start.2 = ((f32[16,1,1280]{2,1,0:T(1,128)}), f32[16,1,1280]{2,1,0:T(1,128)S(1)}, u32[]{:S(2)}, u32[]{:S(2)}) async-start(f32[16,1,1280]{2,1,0:T(1,128)} %shard_map.150), calls=%async_computation.2 | async-start | bytes 163840 | tf_op jit(solution)/shard_map/all_to_all | solution.py:458
  115.6 9.1 %collective-permute-start.1 = (f32[8,256]{1,0:T(8,128)}, f32[8,256]{1,0:T(8,128)S(1)}, u32[]{:S(2)}, u32[]{:S(2)}) collective-permute-start(f32[8,256]{1,0:T(8,128)} %get-tuple-element.28), channel_id=1, source_target_pairs={{8,0},{16,8},{24,16},{32,24},{40,32},{48,40},{56,48},{64,56},{72,6... | collective-permute-start | bytes 24584 | tf_op jit(solution)/shard_map/ppermute | solution.py:374
  123.2 3.6 %collective-permute-start.5 = (f32[8,256]{1,0:T(8,128)S(1)}, f32[8,256]{1,0:T(8,128)S(1)}, u32[]{:S(2)}, u32[]{:S(2)}) collective-permute-start(f32[8,256]{1,0:T(8,128)S(1)} %shard_map.151.mine), channel_id=1, source_target_pairs={{0,8},{8,0},{16,24},{24,16},{32,40},{40,32},{48,56},{56,48},{64,72... | collective-permute-start | bytes 24584 | tf_op jit(solution)/shard_map/ppermute | solution.py:462
  124.7 0.6 copy-start.16

commit v3 on v2

--- a/solution.py
+++ b/solution.py
@@ -117,9 +117,9 @@
     return mm(bh, high) + mm(bh, low) + mm(bl, high)
 
 
-def correlate(blocks, which, src, tab_in, twist_in, out, left, right, tab, twist, sems):
+def correlate(blocks, left_in, src, tab_in, twist_in, out, left, right, tab, twist, sems):
     pairs = (
-        (src.at[:, pl.ds(8 * which, 8)], left),
+        (left_in.at[:, pl.ds(0, 8)], left),
         (src.at[:, pl.ds(8, 8)], right),
         (tab_in, tab),
         (twist_in, twist),
@@ -144,11 +144,11 @@
 
 
 def first_kernel(blocks, src, tab, twist, ahead, out, *scratch):
-    correlate(blocks, 0, src, tab, twist, out, *scratch)
-
-
-def second_kernel(blocks, src, tab, twist, out, held, *scratch):
-    correlate(blocks, 2, src, tab, twist, held, *scratch)
+    correlate(blocks, src, src, tab, twist, out, *scratch)
+
+
+def second_kernel(blocks, kv, src, tab, twist, out, held, *scratch):
+    correlate(blocks, kv, src, tab, twist, held, *scratch)
     for a in range(4 * blocks):
         out[:, a * LANES : (a + 1) * LANES] = held[a * 8 : (a + 1) * 8, :]
 
@@ -166,13 +166,13 @@
     )
 
 
-def edge_kernel(q, k, v, tails):
+def edge_kernel(q, k, v, go, fil, tails):
     for i, x in enumerate((q, k, v)):
         tails[2 * i : 2 * i + 2, :] = x[6:8, :]
     tails[6:8, :] = jnp.zeros((2, q.shape[1]), f32)
 
 
-def send_kernel(t_ref, taps, prev_in, q, k, v, go, fil, out, ext, gof, prev, sems):
+def send_kernel(t_ref, taps, prev, q, k, v, go, fil, out, late, ext, gof, sems):
     n = q.shape[0]
     copies = [
         pltpu.make_async_copy(src, dst, sems.at[i])
@@ -183,28 +183,27 @@
                 (v, ext.at[2, pl.ds(8, n)]),
                 (q, ext.at[0, pl.ds(8, n)]),
                 (go, gof.at[1]),
-                (prev_in, prev),
             )
         )
     ]
     for c in copies:
         c.start()
     t = t_ref[0]
+    for i in range(3):
+        ext[i, 6:8, :] = prev[2 * i : 2 * i + 2, :]
     groups = out.shape[0]
     owners = [owner_of(g, t) for g in range(groups)]
 
     def put(i, r0, piece):
         turned = jnp.transpose(piece)
+        at, dst = (0, late) if i == 2 else (i * 8, out)
         for g in range(groups):
-            out[owners[g], r0 // LANES, i * 8 : i * 8 + 8, :] = turned[g * 8 : g * 8 + 8]
+            dst[owners[g], r0 // LANES, at : at + 8, :] = turned[g * 8 : g * 8 + 8]
 
     starts = range(0, n, LANES)
     copies[0].wait()
     for r0 in starts:
         put(0, r0, gof[0, r0 : r0 + LANES, :])
-    copies[5].wait()
-    for i in range(3):
-        ext[i, 6:8, :] = prev[2 * i : 2 * i + 2, :]
     copies[1].wait()
     copies[2].wait()
     for r0 in starts:
@@ -251,37 +250,21 @@
 
 
 def last_kernel(
-    t_ref, corr, zbase_in, ks_in, vs_in, taps, prev, k, v, early,
-    gk, gv, heads, keep, give, ext, gext, held, base, sems,
+    t_ref, corr, zbase, ks, vs, taps, prev, k, v, early, gk, gv, heads, keep, give, ext, gext, held
 ):
     t = t_ref[0]
     n = k.shape[0]
-    steps = []
-    for j, r0 in enumerate(range(0, n, LANES)):
-        rows = pl.ds(r0, LANES)
-        pairs = [(x.at[rows], base.at[i, rows]) for i, x in enumerate((zbase_in, ks_in, vs_in))]
-        pairs += [
-            (x.at[rows], ext.at[i, pl.ds(8 + r0, LANES)]) for i, x in enumerate((k, v))
-        ]
-        steps.append(
-            [pltpu.make_async_copy(x, y, sems.at[5 * j + i]) for i, (x, y) in enumerate(pairs)]
-        )
-    for step in steps:
-        for c in step:
-            c.start()
-    zbase, ks, vs = base.at[0], base.at[1], base.at[2]
     groups = corr.shape[0]
     owners = [owner_of(g, t) for g in range(groups)]
-    for i in range(2):
+    for i, x in enumerate((k, v)):
         ext[i, 6:8, :] = prev[2 * i + 2 : 2 * i + 4, :]
+        ext[i, 8:, :] = x[...]
         gext[i, n:, :] = jnp.zeros((8, k.shape[1]), f32)
     totals = [jnp.zeros((1, k.shape[1]), f32) for _ in range(6)]
     for r0 in range(0, n, LANES):
         rows = slice(r0, r0 + LANES)
         for g in range(groups):
             held[g * 8 : g * 8 + 8, :] = corr[owners[g], r0 // LANES]
-        for c in steps[r0 // LANES]:
-            c.wait()
         grad_z = zbase[rows, :] + jnp.transpose(held[...])
         for i, other in enumerate((vs, ks)):
             g = grad_z * other[rows, :]
@@ -390,23 +373,23 @@
         edge_kernel,
         grid=(1,),
         out_shape=shape(8, width),
-        in_specs=[low, low, low],
+        in_specs=[low, low, low, top, top],
         out_specs=top,
         name="edge",
-    )(q, k, v)
+    )(q, k, v, go, fil)
     prev = shifted(tails, 1)
 
     ext3 = pltpu.VMEM((3, n + 8, width), f32)
-    packed = call(
-        send_kernel, [SM, VM] + [HB] * 6, shape(blocks, n // LANES, 24, LANES),
+    packed, packed_kv = call(
+        send_kernel, [SM, VM, VM] + [HB] * 5,
+        (shape(blocks, n // LANES, 16, LANES), shape(blocks, n // LANES, 8, LANES)),
         (t, taps, prev, q, k, v, go, fil),
-        [
-            ext3, pltpu.VMEM((2, n, width), f32), pltpu.VMEM((8, width), f32),
-            pltpu.SemaphoreType.DMA((6,)),
-        ], room=62,
+        [ext3, pltpu.VMEM((2, n, width), f32), pltpu.SemaphoreType.DMA((5,))],
     )
     arrived = lax.all_to_all(packed, "ctx", 0, 0, tiled=True)
-    arrived = arrived.reshape(seq // LANES, 24, LANES)
+    arrived_kv = lax.all_to_all(packed_kv, "ctx", 0, 0, tiled=True)
+    arrived = arrived.reshape(seq // LANES, 16, LANES)
+    arrived_kv = arrived_kv.reshape(seq // LANES, 8, LANES)
     work = [
         pltpu.VMEM((seq // LANES, 8, LANES), f32),
         pltpu.VMEM((seq // LANES, 8, LANES), f32),
@@ -422,13 +405,13 @@
     corr = call(
         functools.partial(first_kernel, blocks), [HB, TB, TB, HB],
         shape(seq * 8 // LANES, LANES), (arrived, *tabs, early), work,
-        flops=2 * 10**9, room=62,
+        flops=2 * 10**9, room=58,
     )
     back = lax.all_to_all(corr.reshape(blocks, n // LANES, 8, LANES), "ctx", 0, 0, tiled=True)
     zeta = call(
-        functools.partial(second_kernel, blocks), [HB, TB, TB],
-        shape(8, seq), (arrived, *tabs),
-        [pltpu.VMEM((seq * 8 // LANES, LANES), f32), *work], flops=2 * 10**9, room=62,
+        functools.partial(second_kernel, blocks), [HB, HB, TB, TB],
+        shape(8, seq), (arrived_kv, arrived, *tabs),
+        [pltpu.VMEM((seq * 8 // LANES, LANES), f32), *work], flops=2 * 10**9, room=58,
     )
     hop_one, hop_two = [], []
     for c in range(blocks):
@@ -440,16 +423,14 @@
     grad_filter = lax.ppermute(zeta, ("ctx", "tp"), hop_two)
 
     gk, gv, heads, keep, give = call(
-        last_kernel, [SM, VM, HB, HB, HB, VM, VM, HB, HB, VM],
+        last_kernel, [SM] + [VM] * 9,
         (shape(n, width), shape(n, width), shape(8, width), shape(8, width), shape(8, width)),
         (t, back, zbase, ks, vs, taps, prev, k, v, early),
         [
             pltpu.VMEM((2, n + 8, width), f32),
             pltpu.VMEM((2, n + 8, width), f32),
             pltpu.VMEM((width, LANES), f32),
-            pltpu.VMEM((3, n, width), f32),
-            pltpu.SemaphoreType.DMA((5 * (n // LANES),)),
-        ], room=60,
+        ],
     )
     swap = [(i, i ^ 1) for i in range(blocks)]
     got = lax.ppermute(give, "ctx", swap)

time: 131 us -> 133 us (1.015)
  blocking collectives: 0 us -> 38 us
  waiting for transfers between devices: 46.9 us -> 19 us
  Pallas kernels: 28.3 us -> 24.9 us
  starting transfers between devices: 45.4 us -> 43 us
    all_to_all x0 -> x1, blocking collectives: none -> 38 us  [on_device(): arrived = lax.all_to_all(packed, 'ctx', 0, 0, tiled=True)]
    all_to_all x1, waiting for transfers between devices: 33.3 us -> 5.27 us  [on_device(): arrived_kv = lax.all_to_all(packed_kv, 'ctx', 0, 0, tiled=True)]
    all_to_all x1, starting transfers between devices: 11.7 us -> 6.51 us  [on_device(): arrived_kv = lax.all_to_all(packed_kv, 'ctx', 0, 0, tiled=True)]
    pallas_call x8, Pallas kernels: 25.6 us -> 22 us  [call(): pl.pallas_call(body, out_shape=outs, in_specs=ins, out_specs=jax.tree.map...]
    all_to_all x1, starting transfers between devices: 10.4 us -> 12.5 us  [on_device(): lax.all_to_all(parts, 'ctx', 0, 0, axis_index_groups=same, tiled=True)]
    unnamed x35 -> x31, local copies, waits for them, and re-layouts: 6.53 us -> 5.38 us
  transfers between devices with their start and end apart: 9 -> 9, of which waited for: 5 -> 5; matrix products, arithmetic and copies ran while one was open for 1% -> 0% of each run, Pallas kernels for 12% -> 15%
where the time goes in v3:
time: 133 us; the launch traced here: 131 us
  starting transfers between devices  43 us (32%)
  blocking collectives  38 us (29%)
  Pallas kernels  24.9 us (19%)
  waiting for transfers between devices  19 us (14%)
  local copies, waits for them, and re-layouts  5.38 us (4%)
    all_to_all x1, blocking collectives, on_device(): arrived = lax.all_to_all(packed, 'ctx', 0, 0, tiled=True)  38 us
    pallas_call x8, Pallas kernels, call(): pl.pallas_call(body, out_shape=outs, in_specs=ins, out_specs=jax.tree.map...  22 us
    all_to_all x1, starting transfers between devices, on_device(): lax.all_to_all(parts, 'ctx', 0, 0, axis_index_groups=same, tiled=True)  12.5 us
    ppermute x2, starting transfers between devices, shifted(): return lax.ppermute(value, 'ctx', pairs)  7.58 us
    ppermute x1, starting transfers between devices, on_device(): zeta = lax.ppermute(zeta, ('ctx', 'tp'), hop_one)  6.99 us
    ppermute x1, waiting for transfers between devices, on_device(): zeta = lax.ppermute(zeta, ('ctx', 'tp'), hop_one)  6.76 us
    all_to_all x1, starting transfers between devices, on_device(): arrived_kv = lax.all_to_all(packed_kv, 'ctx', 0, 0, tiled=True)  6.51 us
    all_to_all x1, starting transfers between devices, on_device(): lax.all_to_all(corr.reshape(blocks, n // LANES, 8, LANES), 'ctx', 0, 0, t...  5.6 us
  transfers between devices with their start and end apart: 9, of which 5 were waited for; matrix products, arithmetic and copies ran while one was open for 0% of the time, Pallas kernels for 15%

profile of v3, /device:TPU:1, one launch (start us, length us, event | category | flops | bytes accessed | tf_op | source)
XLA Modules:
  0.0 131.1 jit_solution(8949186568438322805)
XLA Ops:
  0.6 0.0 copy-start.1
  0.6 0.0 copy-start
  0.7 0.0 copy-start.3
  0.7 0.0 copy-start.2
  0.7 0.0 copy-start.4
  0.7 1.5 %edge.1 = f32[8,256]{1,0:T(8,128)} custom-call(f32[512,256]{1,0:T(8,128)} %q.5, f32[512,256]{1,0:T(8,128)} %k.7, f32[512,256]{1,0:T(8,128)} %v.7, f32[512,256]{1,0:T(8,128)} %go.5, f32[512,256]{1,0:T(8,128)} %fil.3), custom_call_target="tpu_custom_call" | custom-call | tf_op jit(solution)/shard_map/edge/pallas_call | solution.py:372
  2.2 5.0 %collective-permute-start = (f32[8,256]{1,0:T(8,128)}, f32[8,256]{1,0:T(8,128)S(1)}, u32[]{:S(2)}, u32[]{:S(2)}) collective-permute-start(f32[8,256]{1,0:T(8,128)} %edge.1), channel_id=1, source_target_pairs={{0,8},{8,16},{16,24},{24,32},{32,40},{40,48},{48,56},{56,64},{64,7... | collective-permute-start | bytes 24584 | tf_op jit(solution)/shard_map/ppermute | solution.py:357
  7.2 0.1 pad_add_fusion.t_ref
  7.3 0.9 collective-permute-done.prev
  8.2 0.0 copy-done.1
  8.2 0.0 copy-done
  8.3 2.3 %shard_map.146 = (f32[32,4,16,128]{3,2,1,0:T(8,128)S(1)}, f32[32,4,8,128]{3,2,1,0:T(8,128)}) custom-call(s32[2]{0:T(128)S(1)} %pad_add_fusion.t_ref, f32[3,3,256]{2,1,0:T(4,128)S(1)} %copy-done.10, f32[8,256]{1,0:T(8,128)S(1)} %collective-permute-done.prev, f32[512,256]{1,0:T(8,128)S(1)} %copy-done.2, f32[512,256]{1,0:T(8,128)S(1)} %copy-done, ...), custom_call_target="tpu_custom_call" | custom-call | flops 1000000 | bytes 4000000 | tf_op jit(solution)/shard_map/pallas_call | solution.py:343
  10.6 38.0 %all_to_all.20 = f32[32,4,16,128]{3,2,1,0:T(8,128)} all-to-all(f32[32,4,16,128]{3,2,1,0:T(8,128)S(1)} %get-tuple-element.24), channel_id=1, replica_groups=mesh['ctx'=32,'tp'=8] {'ctx'}, dimensions={0} | all-to-all | bytes 2097152 | tf_op jit(solution)/shard_map/all_to_all | solution.py:389
  48.5 6.5 %all-to-all-start.2 = ((f32[32,4,8,128]{3,2,1,0:T(8,128)}), f32[32,4,8,128]{3,2,1,0:T(8,128)}, u32[]{:S(2)}, u32[]{:S(2)}) async-start(f32[32,4,8,128]{3,2,1,0:T(8,128)} %get-tuple-element.35), calls=%async_computation.2 | async-start | bytes 1048576 | tf_op jit(solution)/shard_map/all_to_all | solution.py:390
  55.1 0.0 copy-start.13
  55.1 0.7 copy-done.13
  55.8 2.0 %shard_map.145 = (f32[512,256]{1,0:T(8,128)S(1)}, f32[512,256]{1,0:T(8,128)S(1)}, f32[512,256]{1,0:T(8,128)S(1)}, f32[512,256]{1,0:T(8,128)}, f32[8,256]{1,0:T(8,128)S(1)}) custom-call(f32[3,3,256]{2,1,0:T(4,128)S(1)} %copy-done.10, f32[8,256]{1,0:T(8,128)S(1)} %collective-permute-done.prev, f32[512,256]{1,0:T(8,128)S(1)} %copy-done.2, ...), custom_call_target="tpu_custom_call" | custom-call | flops 1000000 | bytes 4000000 | tf_op jit(solution)/shard_map/pallas_call | solution.py:343
  57.7 0.8 copy-done.6
  58.5 0.8 copy-done.8
  59.3 0.6 copy-done.11
  59.9 6.6 %shard_map.147 = f32[1024,128]{1,0:T(8,128)} custom-call(f32[128,16,128]{2,1,0:T(8,128)} %bitcast.8, bf16[1664,256]{1,0:T(8,128)(2,1)} %constant.15.clone.tab, f32[256,128]{1,0:T(8,128)} %constant.16.clone.twist, f32[8,256]{1,0:T(8,128)} %copy-done.11), custom_call_target="tpu_custom_call" | custom-call | flops 2000000000 | bytes 4000000 | tf_op jit(solution)/shard_map/pallas_call | solution.py:343
  66.6 5.3 %all-to-all-done.2 = f32[32,4,8,128]{3,2,1,0:T(8,128)} async-done(((f32[32,4,8,128]{3,2,1,0:T(8,128)}), f32[32,4,8,128]{3,2,1,0:T(8,128)}, u32[]{:S(2)}, u32[]{:S(2)}) %all-to-all-start.2) | async-done | bytes 524320 | tf_op jit(solution)/shard_map/all_to_all | solution.py:390
  71.8 5.6 %all-to-all-start.1 = ((f32[32,4,8,128]{3,2,1,0:T(8,128)}), f32[32,4,8,128]{3,2,1,0:T(8,128)S(1)}, u32[]{:S(2)}, u32[]{:S(2)}) async-start(f32[32,4,8,128]{3,2,1,0:T(8,128)} %bitcast.10), calls=%async_computation.1 | async-start | bytes 1048576 | tf_op jit(solution)/shard_map/all_to_all | solution.py:410
  77.4 0.0 copy-start.7
  77.5 0.0 copy-start.12
  77.5 6.8 %shard_map.149 = f32[8,16384]{1,0:T(8,128)} custom-call(f32[128,8,128]{2,1,0:T(8,128)} %bitcast.5.kv, f32[128,16,128]{2,1,0:T(8,128)} %bitcast.9, bf16[1664,256]{1,0:T(8,128)(2,1)} %constant.15.clone.tab, f32[256,128]{1,0:T(8,128)} %constant.16.clone.twist), custom_call_target="tpu_custom_call" | custom-call | flops 2000000000 | bytes 4000000 | tf_op jit(solution)/shard_map/pallas_call | solution.py:343
  84.3 7.0 %collective-permute-start.2 = (f32[8,16384]{1,0:T(8,128)}, f32[8,16384]{1,0:T(8,128)}, u32[]{:S(2)}, u32[]{:S(2)}) collective-permute-start(f32[8,16384]{1,0:T(8,128)} %shard_map.149), channel_id=1, source_target_pairs={{0,0},{1,2},{2,1},{3,3},{4,4},{5,6},{6,5},{7,7},{8,13},{9,15},{10,... | collective-permute-start | bytes 1572872 | tf_op jit(solution)/shard_map/ppermute | solution.py:422
  91.3 6.8 %collective-permute-done.2 = f32[8,16384]{1,0:T(8,128)} collective-permute-done((f32[8,16384]{1,0:T(8,128)}, f32[8,16384]{1,0:T(8,128)}, u32[]{:S(2)}, u32[]{:S(2)}) %collective-permute-start.2) | collective-permute-done | bytes 524320 | tf_op jit(solution)/shard_map/ppermute | solution.py:422
  98.0 1.9 %collective-permute-start.3 = (f32[8,16384]{1,0:T(8,128)}, f32[8,16384]{1,0:T(8,128)}, u32[]{:S(2)}, u32[]{:S(2)}) collective-permute-start(f32[8,16384]{1,0:T(8,128)} %collective-permute-done.2), channel_id=1, source_target_pairs={{0,0},{2,34},{1,81},{3,115},{4,132},{6,166},{5,213},{7,247},{13,13... | collective-permute-start | bytes 1572872 | tf_op jit(solution)/shard_map/ppermute | solution.py:423
  99.9 0.0 all-to-all-done.1.corr
  99.9 0.0 copy-done.7
  100.0 0.0 copy-done.9
  100.0 0.0 copy-done.12
  100.0 2.4 %shard_map.148 = (f32[512,256]{1,0:T(8,128)}, f32[512,256]{1,0:T(8,128)}, f32[8,256]{1,0:T(8,128)S(1)}, f32[8,256]{1,0:T(8,128)S(1)}, f32[8,256]{1,0:T(8,128)S(1)}) custom-call(s32[2]{0:T(128)S(1)} %pad_add_fusion.t_ref, f32[32,4,8,128]{3,2,1,0:T(8,128)S(1)} %all-to-all-done.1.corr, f32[512,256]{1,0:T(8,128)S(1)} %get-tuple-element.26.zbase, ...), custom_call_target="tpu_custom_call" | custom-call | flops 1000000 | bytes 4000000 | tf_op jit(solution)/shard_map/pallas_call | solution.py:343
  102.4 0.0 collective-permute-start.4
  102.4 1.2 collective-permute-done.4.got
  103.6 0.7 shard_map.150
  104.2 12.5 %all-to-all-start.3 = ((f32[16,1,1280]{2,1,0:T(1,128)}), f32[16,1,1280]{2,1,0:T(1,128)S(1)}, u32[]{:S(2)}, u32[]{:S(2)}) async-start(f32[16,1,1280]{2,1,0:T(1,128)} %shard_map.150), calls=%async_computation.3 | async-start | bytes 163840 | tf_op jit(solution)/shard_map/all_to_all | solution.py:439
  116.8 2.5 %collective-permute-start.1 = (f32[8,256]{1,0:T(8,128)S(1)}, f32[8,256]{1,0:T(8,128)S(1)}, u32[]{:S(2)}, u32[]{:S(2)}) collective-permute-start(f32[8,256]{1,0:T(8,128)S(1)} %get-tuple-element.31), channel_id=1, source_target_pairs={{8,0},{16,8},{24,16},{32,24},{40,32},{48,40},{56,48},{64,56},{72,6... | collective-permute-start | bytes 24584 | tf_op jit(solution)/shard_map/ppermute | solution.py:357
  119.3 4.8 %all-to-all-done.3.parts = f32[16,1,1280]{2,1,0:T(1,128)S(1)} async-done(((f32[16,1,1280]{2,1,0:T(1,128)}), f32[16,1,1280]{2,1,0:T(1,128)S(1)}, u32[]{:S(2)}, u32[]{:S(2)}) %all-to-all-start.3) | async-done | bytes 81952 | tf_op jit(solution)/shard_map/all_to_all | solution.py:439
  124.2 1.9 %collective-permute-start.5 = (f32[8,256]{1,0:T(8,128)S(1)}, f32[8,256]{1,0:T(8,128)S(1)}, u32[]{:S(2)}, u32[]{:S(2)}) collective-permute-start(f32[8,256]{1,0:T(8,128)S(1)} %shard_map.151.mine), channel_id=1, source_target_pairs={{0,8},{8,0},{16,24},{24,16},{32,40},{40,32},{48,56},{56,48},{64,72... | collective-permute-start | bytes 24584 | tf_op jit(solution)/shard_map/ppermute | solution.py:443
  126.0 0.0 collective-permute-done.1.nxt
  126.0 0.6 copy-done.14
  126.6 1.4 %seam.1 = (f32[512,256]{1,0:T(8,128)}, f32[512,256]{1,0:T(8,128)}, f32[512,256]{1,0:T(8,128)}) custom-call(f32[512,256]{1,0:T(8,128)} %get-tuple-element.23.gq_in, f32[512,256]{1,0:T(8,128)} %get-tuple-element.29.gk_in, f32[512,256]{1,0:T(8,128)} %get-tuple-element.30.gv_in, ...), custom_call_target="tpu_custom_call", output_to_operand_aliasing={{0}: (0, {}), {1}: (1, {}), {2}: (2, {})} | custom-call | tf_op jit(solution)/shard_map/seam/pallas_call | solution.py:445
  128.0 0.0 collective-permute-done.3
  128.0 0.0 collective-permute-done.5.other
  128.0 1.2 shard_map.152
  129.2 1.9 %copy.23 = f32[8,16384]{1,0:T(8,128)} copy(f32[8,16384]{1,0:T(8,128)} %collective-permute-done.3) | data formatting | bytes 1048576
  (13 shorter events, 0.0 us)
Async XLA Ops:
  0.6 7.6 %copy-start.1 = (f32[512,256]{1,0:T(8,128)S(1)}, f32[512,256]{1,0:T(8,128)}, u32[]{:S(2)}) copy-start(f32[512,256]{1,0:T(8,128)} %v.7) | copy-start | bytes 1572868
  0.6 7.6 %copy-start = (f32[512,256]{1,0:T(8,128)S(1)}, f32[512,256]{1,0:T(8,128)}, u32[]{:S(2)}) copy-start(f32[512,256]{1,0:T(8,128)} %k.7) | copy-start | bytes 1572868
  0.7 7.6 %copy-start.3 = (f32[512,256]{1,0:T(8,128)S(1)}, f32[512,256]{1,0:T(8,128)}, u32[]{:S(2)}) copy-start(f32[512,256]{1,0:T(8,128)} %go.5) | copy-start | bytes 1572868
  0.7 7.6 %copy-start.2 = (f32[512,256]{1,0:T(8,128)S(1)}, f32[512,256]{1,0:T(8,128)}, u32[]{:S(2)}) copy-start(f32[512,256]{1,0:T(8,128)} %q.5) | copy-start | bytes 1572868
  0.7 7.6 %copy-start.4 = (f32[512,256]{1,0:T(8,128)S(1)}, f32[512,256]{1,0:T(8,128)}, u32[]{:S(2)}) copy-start(f32[512,256]{1,0:T(8,128)} %fil.3) | copy-start | bytes 1572868
  2.2 6.1 %copy-start.10 = (f32[3,3,256]{2,1,0:T(4,128)S(1)}, f32[3,3,256]{2,1,0:T(4,128)}, u32[]{:S(2)}) copy-start(f32[3,3,256]{2,1,0:T(4,128)} %taps.7) | copy-start | bytes 27652
  2.2 6.0 %collective-permute-start = (f32[8,256]{1,0:T(8,128)}, f32[8,256]{1,0:T(8,128)S(1)}, u32[]{:S(2)}, u32[]{:S(2)}) collective-permute-start(f32[8,256]{1,0:T(8,128)} %edge.1), channel_id=1, source_target_pairs={{0,8},{8,16},{16,24},{24,32},{32,40},{40,48},{48,56},{56,64},{64,7... | collective-permute-start | bytes 24584 | tf_op jit(solution)/shard_map/ppermute | solution.py:357
  48.5 6.5 %copy-start.5 = (f32[512,256]{1,0:T(8,128)S(1)}, f32[512,256]{1,0:T(8,128)}, u32[]{:S(2)}) copy-start(f32[512,256]{1,0:T(8,128)} %cs.1) | copy-start | bytes 1572868
  48.5 23.3 %all-to-all-start.2 = ((f32[32,4,8,128]{3,2,1,0:T(8,128)}), f32[32,4,8,128]{3,2,1,0:T(8,128)}, u32[]{:S(2)}, u32[]{:S(2)}) async-start(f32[32,4,8,128]{3,2,1,0:T(8,128)} %get-tuple-element.35), calls=%async_computation.2 | async-start | bytes 1048576 | tf_op jit(solution)/shard_map/all_to_all | solution.py:390
  55.1 0.7 copy-start.13
  57.7 0.8 copy-start.6
  58.5 0.8 copy-start.8
  59.3 0.6 copy-start.11
  71.8 28.1 %all-to-all-start.1 = ((f32[32,4,8,128]{3,2,1,0:T(8,128)}), f32[32,4,8,128]{3,2,1,0:T(8,128)S(1)}, u32[]{:S(2)}, u32[]{:S(2)}) async-start(f32[32,4,8,128]{3,2,1,0:T(8,128)} %bitcast.10), calls=%async_computation.1 | async-start | bytes 1048576 | tf_op jit(solution)/shard_map/all_to_all | solution.py:410
  77.4 22.5 %copy-start.7 = (f32[512,256]{1,0:T(8,128)S(1)}, f32[512,256]{1,0:T(8,128)}, u32[]{:S(2)}) copy-start(f32[512,256]{1,0:T(8,128)} %copy-done.6) | copy-start | bytes 1572868
  77.5 22.5 %copy-start.9 = (f32[512,256]{1,0:T(8,128)S(1)}, f32[512,256]{1,0:T(8,128)}, u32[]{:S(2)}) copy-start(f32[512,256]{1,0:T(8,128)} %copy-done.8) | copy-start | bytes 1572868
  77.5 22.5 %copy-start.12 = (f32[8,256]{1,0:T(8,128)S(1)}, f32[8,256]{1,0:T(8,128)}, u32[]{:S(2)}) copy-start(f32[8,256]{1,0:T(8,128)} %copy-done.11) | copy-start | bytes 24580
  84.3 13.8 %collective-permute-start.2 = (f32[8,16384]{1,0:T(8,128)}, f32[8,16384]{1,0:T(8,128)}, u32[]{:S(2)}, u32[]{:S(2)}) collective-permute-start(f32[8,16384]{1,0:T(8,128)} %shard_map.149), channel_id=1, source_target_pairs={{0,0},{1,2},{2,1},{3,3},{4,4},{5,6},{6,5},{7,7},{8,13},{9,15},{10,... | collective-permute-start | bytes 1572872 | tf_op jit(solution)/shard_map/ppermute | solution.py:422
  98.0 30.0 %collective-permute-start.3 = (f32[8,16384]{1,0:T(8,128)}, f32[8,16384]{1,0:T(8,128)}, u32[]{:S(2)}, u32[]{:S(2)}) collective-permute-start(f32[8,16384]{1,0:T(8,128)} %collective-permute-done.2), channel_id=1, source_target_pairs={{0,0},{2,34},{1,81},{3,115},{4,132},{6,166},{5,213},{7,247},{13,13... | collective-permute-start | bytes 1572872 | tf_op jit(solution)/shard_map/ppermute | solution.py:423
  102.4 1.2 collective-permute-start.4
  104.2 19.9 %all-to-all-start.3 = ((f32[16,1,1280]{2,1,0:T(1,128)}), f32[16,1,1280]{2,1,0:T(1,128)S(1)}, u32[]{:S(2)}, u32[]{:S(2)}) async-start(f32[16,1,1280]{2,1,0:T(1,128)} %shard_map.150), calls=%async_computation.3 | async-start | bytes 163840 | tf_op jit(solution)/shard_map/all_to_all | solution.py:439
  116.8 9.3 %collective-permute-start.1 = (f32[8,256]{1,0:T(8,128)S(1)}, f32[8,256]{1,0:T(8,128)S(1)}, u32[]{:S(2)}, u32[]{:S(2)}) collective-permute-start(f32[8,256]{1,0:T(8,128)S(1)} %get-tuple-element.31), channel_id=1, source_target_pairs={{8,0},{16,8},{24,16},{32,24},{40,32},{48,40},{56,48},{64,56},{72,6... | collective-permute-start | bytes 24584 | tf_op jit(solution)/shard_map/ppermute | solution.py:357
  124.2 3.9 %collective-permute-start.5 = (f32[8,256]{1,0:T(8,128)S(1)}, f32[8,256]{1,0:T(8,128)S(1)}, u32[]{:S(2)}, u32[]{:S(2)}) collective-permute-start(f32[8,256]{1,0:T(8,128)S(1)} %shard_map.151.mine), channel_id=1, source_target_pairs={{0,8},{8,0},{16,24},{24,16},{32,40},{40,32},{48,56},{56,48},{64,72... | collective-permute-start | bytes 24584 | tf_op jit(solution)/shard_map/ppermute | solution.py:443
  126.0 0.6 copy-start.14

commit v4 on v3

--- a/solution.py
+++ b/solution.py
@@ -117,9 +117,9 @@
     return mm(bh, high) + mm(bh, low) + mm(bl, high)
 
 
-def correlate(blocks, left_in, src, tab_in, twist_in, out, left, right, tab, twist, sems):
+def correlate(blocks, which, src, tab_in, twist_in, out, left, right, tab, twist, sems):
     pairs = (
-        (left_in.at[:, pl.ds(0, 8)], left),
+        (src.at[:, pl.ds(8 * which, 8)], left),
         (src.at[:, pl.ds(8, 8)], right),
         (tab_in, tab),
         (twist_in, twist),
@@ -144,11 +144,11 @@
 
 
 def first_kernel(blocks, src, tab, twist, ahead, out, *scratch):
-    correlate(blocks, src, src, tab, twist, out, *scratch)
-
-
-def second_kernel(blocks, kv, src, tab, twist, out, held, *scratch):
-    correlate(blocks, kv, src, tab, twist, held, *scratch)
+    correlate(blocks, 0, src, tab, twist, out, *scratch)
+
+
+def second_kernel(blocks, src, tab, twist, out, held, *scratch):
+    correlate(blocks, 2, src, tab, twist, held, *scratch)
     for a in range(4 * blocks):
         out[:, a * LANES : (a + 1) * LANES] = held[a * 8 : (a + 1) * 8, :]
 
@@ -172,7 +172,7 @@
     tails[6:8, :] = jnp.zeros((2, q.shape[1]), f32)
 
 
-def send_kernel(t_ref, taps, prev, q, k, v, go, fil, out, late, ext, gof, sems):
+def send_kernel(t_ref, taps, prev, q, k, v, go, fil, out, ext, gof, sems):
     n = q.shape[0]
     copies = [
         pltpu.make_async_copy(src, dst, sems.at[i])
@@ -196,9 +196,8 @@
 
     def put(i, r0, piece):
         turned = jnp.transpose(piece)
-        at, dst = (0, late) if i == 2 else (i * 8, out)
         for g in range(groups):
-            dst[owners[g], r0 // LANES, at : at + 8, :] = turned[g * 8 : g * 8 + 8]
+            out[owners[g], r0 // LANES, i * 8 : i * 8 + 8, :] = turned[g * 8 : g * 8 + 8]
 
     starts = range(0, n, LANES)
     copies[0].wait()
@@ -380,16 +379,13 @@
     prev = shifted(tails, 1)
 
     ext3 = pltpu.VMEM((3, n + 8, width), f32)
-    packed, packed_kv = call(
-        send_kernel, [SM, VM, VM] + [HB] * 5,
-        (shape(blocks, n // LANES, 16, LANES), shape(blocks, n // LANES, 8, LANES)),
+    packed = call(
+        send_kernel, [SM, VM, VM] + [HB] * 5, shape(blocks, n // LANES, 24, LANES),
         (t, taps, prev, q, k, v, go, fil),
         [ext3, pltpu.VMEM((2, n, width), f32), pltpu.SemaphoreType.DMA((5,))],
     )
     arrived = lax.all_to_all(packed, "ctx", 0, 0, tiled=True)
-    arrived_kv = lax.all_to_all(packed_kv, "ctx", 0, 0, tiled=True)
-    arrived = arrived.reshape(seq // LANES, 16, LANES)
-    arrived_kv = arrived_kv.reshape(seq // LANES, 8, LANES)
+    arrived = arrived.reshape(seq // LANES, 24, LANES)
     work = [
         pltpu.VMEM((seq // LANES, 8, LANES), f32),
         pltpu.VMEM((seq // LANES, 8, LANES), f32),
@@ -409,8 +405,8 @@
     )
     back = lax.all_to_all(corr.reshape(blocks, n // LANES, 8, LANES), "ctx", 0, 0, tiled=True)
     zeta = call(
-        functools.partial(second_kernel, blocks), [HB, HB, TB, TB],
-        shape(8, seq), (arrived_kv, arrived, *tabs),
+        functools.partial(second_kernel, blocks), [HB, TB, TB],
+        shape(8, seq), (arrived, *tabs),
         [pltpu.VMEM((seq * 8 // LANES, LANES), f32), *work], flops=2 * 10**9, room=58,
     )
     hop_one, hop_two = [], []

time: 133 us -> 128 us (0.962)
  blocking collectives: 38 us -> 0 us
  waiting for transfers between devices: 19 us -> 47.8 us
  starting transfers between devices: 43 us -> 47.9 us
    all_to_all x1 -> x0, blocking collectives: 38 us -> none  [on_device(): arrived = lax.all_to_all(packed, 'ctx', 0, 0, tiled=True)]
    all_to_all x1, waiting for transfers between devices: 5.27 us -> 34.1 us  [on_device(): arrived = lax.all_to_all(packed, 'ctx', 0, 0, tiled=True)]
    all_to_all x1, starting transfers between devices: 6.51 us -> 11.7 us  [on_device(): arrived = lax.all_to_all(packed, 'ctx', 0, 0, tiled=True)]
  transfers between devices with their start and end apart: 9 -> 9, of which waited for: 5 -> 5; matrix products, arithmetic and copies ran while one was open for 0% -> 0% of each run, Pallas kernels for 15% -> 10%
where the time goes in v4:
time: 128 us; the launch traced here: 127 us
  starting transfers between devices  47.9 us (37%)
  waiting for transfers between devices  47.8 us (37%)
  Pallas kernels  25.4 us (20%)
  local copies, waits for them, and re-layouts  4.71 us (4%)
    all_to_all x1, waiting for transfers between devices, on_device(): arrived = lax.all_to_all(packed, 'ctx', 0, 0, tiled=True)  34.1 us
    pallas_call x8, Pallas kernels, call(): pl.pallas_call(body, out_shape=outs, in_specs=ins, out_specs=jax.tree.map...  22.5 us
    all_to_all x1, starting transfers between devices, on_device(): lax.all_to_all(parts, 'ctx', 0, 0, axis_index_groups=same, tiled=True)  12.5 us
    all_to_all x1, starting transfers between devices, on_device(): arrived = lax.all_to_all(packed, 'ctx', 0, 0, tiled=True)  11.7 us
    ppermute x2, starting transfers between devices, shifted(): return lax.ppermute(value, 'ctx', pairs)  7.44 us
    ppermute x1, starting transfers between devices, on_device(): zeta = lax.ppermute(zeta, ('ctx', 'tp'), hop_one)  6.99 us
    ppermute x1, waiting for transfers between devices, on_device(): zeta = lax.ppermute(zeta, ('ctx', 'tp'), hop_one)  6.73 us
    all_to_all x1, starting transfers between devices, on_device(): lax.all_to_all(corr.reshape(blocks, n // LANES, 8, LANES), 'ctx', 0, 0, t...  5.45 us
  transfers between devices with their start and end apart: 9, of which 5 were waited for; matrix products, arithmetic and copies ran while one was open for 0% of the time, Pallas kernels for 10%

profile of v4, /device:TPU:1, one launch (start us, length us, event | category | flops | bytes accessed | tf_op | source)
XLA Modules:
  0.0 126.7 jit_solution(13754478156021752292)
XLA Ops:
  0.6 0.0 copy-start.1
  0.6 0.0 copy-start
  0.7 0.0 copy-start.3
  0.7 0.0 copy-start.2
  0.7 0.0 copy-start.4
  0.7 0.0 copy-start.10
  0.7 1.5 %edge.1 = f32[8,256]{1,0:T(8,128)} custom-call(f32[512,256]{1,0:T(8,128)} %q.5, f32[512,256]{1,0:T(8,128)} %k.7, f32[512,256]{1,0:T(8,128)} %v.7, f32[512,256]{1,0:T(8,128)} %go.5, f32[512,256]{1,0:T(8,128)} %fil.3), custom_call_target="tpu_custom_call" | custom-call | tf_op jit(solution)/shard_map/edge/pallas_call | solution.py:371
  2.2 4.9 %collective-permute-start = (f32[8,256]{1,0:T(8,128)}, f32[8,256]{1,0:T(8,128)S(1)}, u32[]{:S(2)}, u32[]{:S(2)}) collective-permute-start(f32[8,256]{1,0:T(8,128)} %edge.1), channel_id=1, source_target_pairs={{0,8},{8,16},{16,24},{24,32},{32,40},{40,48},{48,56},{56,64},{64,7... | collective-permute-start | bytes 24584 | tf_op jit(solution)/shard_map/ppermute | solution.py:356
  7.1 0.1 pad_add_fusion.t_ref
  7.2 0.9 collective-permute-done.prev
  8.1 0.0 copy-done.1
  8.1 2.8 %shard_map.146 = f32[32,4,24,128]{3,2,1,0:T(8,128)} custom-call(s32[2]{0:T(128)S(1)} %pad_add_fusion.t_ref, f32[3,3,256]{2,1,0:T(4,128)S(1)} %copy-done.10, f32[8,256]{1,0:T(8,128)S(1)} %collective-permute-done.prev, f32[512,256]{1,0:T(8,128)S(1)} %copy-done.2, f32[512,256]{1,0:T(8,128)S(1)} %copy-done, f32[512,256]{1,0:T(8,128)S(1)} %copy-done.1, ...), custom_call_target="tpu_custom_call" | custom-call | flops 1000000 | bytes 4000000 | tf_op jit(solution)/shard_map/pallas_call | solution.py:342
  10.9 0.0 copy-start.5
  10.9 0.0 copy-start.13
  10.9 11.7 %all-to-all-start = ((f32[32,4,24,128]{3,2,1,0:T(8,128)}), f32[32,4,24,128]{3,2,1,0:T(8,128)}, u32[]{:S(2)}, u32[]{:S(2)}) async-start(f32[32,4,24,128]{3,2,1,0:T(8,128)} %shard_map.146), calls=%async_computation | async-start | bytes 3145728 | tf_op jit(solution)/shard_map/all_to_all | solution.py:387
  22.7 2.0 %shard_map.145 = (f32[512,256]{1,0:T(8,128)S(1)}, f32[512,256]{1,0:T(8,128)S(1)}, f32[512,256]{1,0:T(8,128)S(1)}, f32[512,256]{1,0:T(8,128)}, f32[8,256]{1,0:T(8,128)S(1)}) custom-call(f32[3,3,256]{2,1,0:T(4,128)S(1)} %copy-done.10, f32[8,256]{1,0:T(8,128)S(1)} %collective-permute-done.prev, f32[512,256]{1,0:T(8,128)S(1)} %copy-done.2, ...), custom_call_target="tpu_custom_call" | custom-call | flops 1000000 | bytes 4000000 | tf_op jit(solution)/shard_map/pallas_call | solution.py:342
  24.7 0.8 copy-done.6
  25.5 0.8 copy-done.8
  26.2 0.6 copy-done.11
  26.8 34.1 %all-to-all-done = f32[32,4,24,128]{3,2,1,0:T(8,128)} async-done(((f32[32,4,24,128]{3,2,1,0:T(8,128)}), f32[32,4,24,128]{3,2,1,0:T(8,128)}, u32[]{:S(2)}, u32[]{:S(2)}) %all-to-all-start) | async-done | bytes 1572896 | tf_op jit(solution)/shard_map/all_to_all | solution.py:387
  60.9 6.7 %shard_map.147 = f32[1024,128]{1,0:T(8,128)} custom-call(f32[128,24,128]{2,1,0:T(8,128)} %bitcast.3.src, bf16[1664,256]{1,0:T(8,128)(2,1)} %constant.15.clone.tab, f32[256,128]{1,0:T(8,128)} %constant.16.clone.twist, f32[8,256]{1,0:T(8,128)} %copy-done.11), custom_call_target="tpu_custom_call" | custom-call | flops 2000000000 | bytes 4000000 | tf_op jit(solution)/shard_map/pallas_call | solution.py:342
  67.6 5.5 %all-to-all-start.1 = ((f32[32,4,8,128]{3,2,1,0:T(8,128)}), f32[32,4,8,128]{3,2,1,0:T(8,128)S(1)}, u32[]{:S(2)}, u32[]{:S(2)}) async-start(f32[32,4,8,128]{3,2,1,0:T(8,128)} %bitcast.7), calls=%async_computation.1 | async-start | bytes 1048576 | tf_op jit(solution)/shard_map/all_to_all | solution.py:406
  73.1 0.0 copy-start.7
  73.1 0.0 copy-start.9
  73.1 0.0 copy-start.12
  73.1 6.8 %shard_map.149 = f32[8,16384]{1,0:T(8,128)} custom-call(f32[128,24,128]{2,1,0:T(8,128)} %bitcast.3.src, bf16[1664,256]{1,0:T(8,128)(2,1)} %constant.15.clone.tab, f32[256,128]{1,0:T(8,128)} %constant.16.clone.twist), custom_call_target="tpu_custom_call" | custom-call | flops 2000000000 | bytes 4000000 | tf_op jit(solution)/shard_map/pallas_call | solution.py:342
  79.9 7.0 %collective-permute-start.2 = (f32[8,16384]{1,0:T(8,128)}, f32[8,16384]{1,0:T(8,128)}, u32[]{:S(2)}, u32[]{:S(2)}) collective-permute-start(f32[8,16384]{1,0:T(8,128)} %shard_map.149), channel_id=1, source_target_pairs={{0,0},{1,2},{2,1},{3,3},{4,4},{5,6},{6,5},{7,7},{8,13},{9,15},{10,... | collective-permute-start | bytes 1572872 | tf_op jit(solution)/shard_map/ppermute | solution.py:418
  86.9 6.7 %collective-permute-done.2 = f32[8,16384]{1,0:T(8,128)} collective-permute-done((f32[8,16384]{1,0:T(8,128)}, f32[8,16384]{1,0:T(8,128)}, u32[]{:S(2)}, u32[]{:S(2)}) %collective-permute-start.2) | collective-permute-done | bytes 524320 | tf_op jit(solution)/shard_map/ppermute | solution.py:418
  93.6 1.9 %collective-permute-start.3 = (f32[8,16384]{1,0:T(8,128)}, f32[8,16384]{1,0:T(8,128)}, u32[]{:S(2)}, u32[]{:S(2)}) collective-permute-start(f32[8,16384]{1,0:T(8,128)} %collective-permute-done.2), channel_id=1, source_target_pairs={{0,0},{2,34},{1,81},{3,115},{4,132},{6,166},{5,213},{7,247},{13,13... | collective-permute-start | bytes 1572872 | tf_op jit(solution)/shard_map/ppermute | solution.py:419
  95.6 0.0 all-to-all-done.1.corr
  95.6 0.0 copy-done.7
  95.6 0.0 copy-done.9
  95.6 0.0 copy-done.12
  95.6 2.4 %shard_map.148 = (f32[512,256]{1,0:T(8,128)}, f32[512,256]{1,0:T(8,128)}, f32[8,256]{1,0:T(8,128)S(1)}, f32[8,256]{1,0:T(8,128)S(1)}, f32[8,256]{1,0:T(8,128)S(1)}) custom-call(s32[2]{0:T(128)S(1)} %pad_add_fusion.t_ref, f32[32,4,8,128]{3,2,1,0:T(8,128)S(1)} %all-to-all-done.1.corr, f32[512,256]{1,0:T(8,128)S(1)} %get-tuple-element.23.zbase, ...), custom_call_target="tpu_custom_call" | custom-call | flops 1000000 | bytes 4000000 | tf_op jit(solution)/shard_map/pallas_call | solution.py:342
  98.0 0.0 collective-permute-start.4
  98.0 1.2 collective-permute-done.4.got
  99.2 0.7 shard_map.150
  99.9 12.5 %all-to-all-start.2 = ((f32[16,1,1280]{2,1,0:T(1,128)}), f32[16,1,1280]{2,1,0:T(1,128)S(1)}, u32[]{:S(2)}, u32[]{:S(2)}) async-start(f32[16,1,1280]{2,1,0:T(1,128)} %shard_map.150), calls=%async_computation.2 | async-start | bytes 163840 | tf_op jit(solution)/shard_map/all_to_all | solution.py:435
  112.4 2.5 %collective-permute-start.1 = (f32[8,256]{1,0:T(8,128)S(1)}, f32[8,256]{1,0:T(8,128)S(1)}, u32[]{:S(2)}, u32[]{:S(2)}) collective-permute-start(f32[8,256]{1,0:T(8,128)S(1)} %get-tuple-element.28), channel_id=1, source_target_pairs={{8,0},{16,8},{24,16},{32,24},{40,32},{48,40},{56,48},{64,56},{72,6... | collective-permute-start | bytes 24584 | tf_op jit(solution)/shard_map/ppermute | solution.py:356
  114.9 4.8 %all-to-all-done.2.parts = f32[16,1,1280]{2,1,0:T(1,128)S(1)} async-done(((f32[16,1,1280]{2,1,0:T(1,128)}), f32[16,1,1280]{2,1,0:T(1,128)S(1)}, u32[]{:S(2)}, u32[]{:S(2)}) %all-to-all-start.2) | async-done | bytes 81952 | tf_op jit(solution)/shard_map/all_to_all | solution.py:435
  119.8 1.9 %collective-permute-start.5 = (f32[8,256]{1,0:T(8,128)S(1)}, f32[8,256]{1,0:T(8,128)S(1)}, u32[]{:S(2)}, u32[]{:S(2)}) collective-permute-start(f32[8,256]{1,0:T(8,128)S(1)} %shard_map.151.mine), channel_id=1, source_target_pairs={{0,8},{8,0},{16,24},{24,16},{32,40},{40,32},{48,56},{56,48},{64,72... | collective-permute-start | bytes 24584 | tf_op jit(solution)/shard_map/ppermute | solution.py:439
  121.6 0.0 collective-permute-done.1.nxt
  121.6 0.6 copy-done.14
  122.2 1.4 %seam.1 = (f32[512,256]{1,0:T(8,128)}, f32[512,256]{1,0:T(8,128)}, f32[512,256]{1,0:T(8,128)}) custom-call(f32[512,256]{1,0:T(8,128)} %get-tuple-element.21.gq_in, f32[512,256]{1,0:T(8,128)} %get-tuple-element.26.gk_in, f32[512,256]{1,0:T(8,128)} %get-tuple-element.27.gv_in, ...), custom_call_target="tpu_custom_call", output_to_operand_aliasing={{0}: (0, {}), {1}: (1, {}), {2}: (2, {})} | custom-call | tf_op jit(solution)/shard_map/seam/pallas_call | solution.py:441
  123.6 0.0 collective-permute-done.3
  123.6 0.0 collective-permute-done.5.other
  123.6 1.2 shard_map.152
  124.8 1.9 %copy.23 = f32[8,16384]{1,0:T(8,128)} copy(f32[8,16384]{1,0:T(8,128)} %collective-permute-done.3) | data formatting | bytes 1048576
  (12 shorter events, 0.0 us)
Async XLA Ops:
  0.6 7.5 %copy-start.1 = (f32[512,256]{1,0:T(8,128)S(1)}, f32[512,256]{1,0:T(8,128)}, u32[]{:S(2)}) copy-start(f32[512,256]{1,0:T(8,128)} %v.7) | copy-start | bytes 1572868
  0.6 7.4 %copy-start = (f32[512,256]{1,0:T(8,128)S(1)}, f32[512,256]{1,0:T(8,128)}, u32[]{:S(2)}) copy-start(f32[512,256]{1,0:T(8,128)} %k.7) | copy-start | bytes 1572868
  0.7 7.4 %copy-start.3 = (f32[512,256]{1,0:T(8,128)S(1)}, f32[512,256]{1,0:T(8,128)}, u32[]{:S(2)}) copy-start(f32[512,256]{1,0:T(8,128)} %go.5) | copy-start | bytes 1572868
  0.7 7.4 %copy-start.2 = (f32[512,256]{1,0:T(8,128)S(1)}, f32[512,256]{1,0:T(8,128)}, u32[]{:S(2)}) copy-start(f32[512,256]{1,0:T(8,128)} %q.5) | copy-start | bytes 1572868
  0.7 7.4 %copy-start.4 = (f32[512,256]{1,0:T(8,128)S(1)}, f32[512,256]{1,0:T(8,128)}, u32[]{:S(2)}) copy-start(f32[512,256]{1,0:T(8,128)} %fil.3) | copy-start | bytes 1572868
  0.7 7.4 %copy-start.10 = (f32[3,3,256]{2,1,0:T(4,128)S(1)}, f32[3,3,256]{2,1,0:T(4,128)}, u32[]{:S(2)}) copy-start(f32[3,3,256]{2,1,0:T(4,128)} %taps.7) | copy-start | bytes 27652
  2.2 5.9 %collective-permute-start = (f32[8,256]{1,0:T(8,128)}, f32[8,256]{1,0:T(8,128)S(1)}, u32[]{:S(2)}, u32[]{:S(2)}) collective-permute-start(f32[8,256]{1,0:T(8,128)} %edge.1), channel_id=1, source_target_pairs={{0,8},{8,16},{16,24},{24,32},{32,40},{40,48},{48,56},{56,64},{64,7... | collective-permute-start | bytes 24584 | tf_op jit(solution)/shard_map/ppermute | solution.py:356
  10.9 11.8 %copy-start.5 = (f32[512,256]{1,0:T(8,128)S(1)}, f32[512,256]{1,0:T(8,128)}, u32[]{:S(2)}) copy-start(f32[512,256]{1,0:T(8,128)} %cs.1) | copy-start | bytes 1572868
  10.9 11.7 %copy-start.13 = (f32[256]{0:T(256)S(1)}, f32[256]{0:T(256)}, u32[]{:S(2)}) copy-start(f32[256]{0:T(256)} %param.15) | copy-start | bytes 3076
  10.9 50.0 %all-to-all-start = ((f32[32,4,24,128]{3,2,1,0:T(8,128)}), f32[32,4,24,128]{3,2,1,0:T(8,128)}, u32[]{:S(2)}, u32[]{:S(2)}) async-start(f32[32,4,24,128]{3,2,1,0:T(8,128)} %shard_map.146), calls=%async_computation | async-start | bytes 3145728 | tf_op jit(solution)/shard_map/all_to_all | solution.py:387
  24.7 0.8 copy-start.6
  25.4 0.8 copy-start.8
  26.2 0.6 copy-start.11
  67.6 28.0 %all-to-all-start.1 = ((f32[32,4,8,128]{3,2,1,0:T(8,128)}), f32[32,4,8,128]{3,2,1,0:T(8,128)S(1)}, u32[]{:S(2)}, u32[]{:S(2)}) async-start(f32[32,4,8,128]{3,2,1,0:T(8,128)} %bitcast.7), calls=%async_computation.1 | async-start | bytes 1048576 | tf_op jit(solution)/shard_map/all_to_all | solution.py:406
  73.1 22.5 %copy-start.7 = (f32[512,256]{1,0:T(8,128)S(1)}, f32[512,256]{1,0:T(8,128)}, u32[]{:S(2)}) copy-start(f32[512,256]{1,0:T(8,128)} %copy-done.6) | copy-start | bytes 1572868
  73.1 22.5 %copy-start.9 = (f32[512,256]{1,0:T(8,128)S(1)}, f32[512,256]{1,0:T(8,128)}, u32[]{:S(2)}) copy-start(f32[512,256]{1,0:T(8,128)} %copy-done.8) | copy-start | bytes 1572868
  73.1 22.5 %copy-start.12 = (f32[8,256]{1,0:T(8,128)S(1)}, f32[8,256]{1,0:T(8,128)}, u32[]{:S(2)}) copy-start(f32[8,256]{1,0:T(8,128)} %copy-done.11) | copy-start | bytes 24580
  79.9 13.7 %collective-permute-start.2 = (f32[8,16384]{1,0:T(8,128)}, f32[8,16384]{1,0:T(8,128)}, u32[]{:S(2)}, u32[]{:S(2)}) collective-permute-start(f32[8,16384]{1,0:T(8,128)} %shard_map.149), channel_id=1, source_target_pairs={{0,0},{1,2},{2,1},{3,3},{4,4},{5,6},{6,5},{7,7},{8,13},{9,15},{10,... | collective-permute-start | bytes 1572872 | tf_op jit(solution)/shard_map/ppermute | solution.py:418
  93.6 30.0 %collective-permute-start.3 = (f32[8,16384]{1,0:T(8,128)}, f32[8,16384]{1,0:T(8,128)}, u32[]{:S(2)}, u32[]{:S(2)}) collective-permute-start(f32[8,16384]{1,0:T(8,128)} %collective-permute-done.2), channel_id=1, source_target_pairs={{0,0},{2,34},{1,81},{3,115},{4,132},{6,166},{5,213},{7,247},{13,13... | collective-permute-start | bytes 1572872 | tf_op jit(solution)/shard_map/ppermute | solution.py:419
  98.0 1.2 collective-permute-start.4
  99.9 19.9 %all-to-all-start.2 = ((f32[16,1,1280]{2,1,0:T(1,128)}), f32[16,1,1280]{2,1,0:T(1,128)S(1)}, u32[]{:S(2)}, u32[]{:S(2)}) async-start(f32[16,1,1280]{2,1,0:T(1,128)} %shard_map.150), calls=%async_computation.2 | async-start | bytes 163840 | tf_op jit(solution)/shard_map/all_to_all | solution.py:435
  112.4 9.3 %collective-permute-start.1 = (f32[8,256]{1,0:T(8,128)S(1)}, f32[8,256]{1,0:T(8,128)S(1)}, u32[]{:S(2)}, u32[]{:S(2)}) collective-permute-start(f32[8,256]{1,0:T(8,128)S(1)} %get-tuple-element.28), channel_id=1, source_target_pairs={{8,0},{16,8},{24,16},{32,24},{40,32},{48,40},{56,48},{64,56},{72,6... | collective-permute-start | bytes 24584 | tf_op jit(solution)/shard_map/ppermute | solution.py:356
  119.8 3.9 %collective-permute-start.5 = (f32[8,256]{1,0:T(8,128)S(1)}, f32[8,256]{1,0:T(8,128)S(1)}, u32[]{:S(2)}, u32[]{:S(2)}) collective-permute-start(f32[8,256]{1,0:T(8,128)S(1)} %shard_map.151.mine), channel_id=1, source_target_pairs={{0,8},{8,0},{16,24},{24,16},{32,40},{40,32},{48,56},{56,48},{64,72... | collective-permute-start | bytes 24584 | tf_op jit(solution)/shard_map/ppermute | solution.py:439
  121.6 0.6 copy-start.14
